TPU v7x, 32 devices: a whole 2x2x4 slice. The times are simulated.
32 devices in a mesh: dp: 4 (over z), section: 2 (over core), tensor: 4 (over y, x).
Axes of the slice: x: 2, y: 2, z: 4, core: 2. Of those that a mesh axis runs over, the one named last changes fastest.
Arguments:
- tokens: bfloat16 [1024, 8192], P('dp', 'tensor'), may hold values from -6 to 6
- dest_slot: int32 [1024], P('dp'), may hold values from 0 to 1023, as said below
- doc_reset: int32 [1024], P('dp'), may hold values 0 or 1
- norm_gain: float32 [2, 8192], P('section'), may hold values from 0.25 to 1.75
- w_in: bfloat16 [2, 8192, 5120], P('section', 'dp', 'tensor'), may hold values from -0.0625 to 0.0625
- w_step: bfloat16 [2, 8192, 32], P('section', None, 'tensor'), may hold values from -0.0625 to 0.0625
- step_bias: float32 [2, 32], P('section', 'tensor'), may hold values from -4 to -1.5
- a_log: float32 [2, 32], P('section', 'tensor'), may hold values from -2.5 to 1.5
- d_skip: float32 [2, 32], P('section', 'tensor'), may hold values from 0.3 to 2
- out_gain: float32 [2, 2048], P('section', 'tensor'), may hold values from 0.25 to 1.75
- w_out: bfloat16 [2, 2048, 8192], P('section', 'tensor'), may hold values from -0.125 to 0.125
Outputs:
- phase_out: bfloat16 [2, 1024, 8192], P('section', 'dp', 'tensor')
Inputs may be any that keep to these rules, and one draw needn't show every extreme that they name: dest_slot is a permutation; the tokens of one group go in order to increasing groups, and each group receives rows in order of source group. One group sends at most 128 tokens to one group, and every group sends exactly 128 to some group.
All inputs are finite; a program needn't handle non-finite values. No bound on the sum of `doc_reset` on one device may be relied on, other than what follows from the above.
Results may differ from a plain program's by a relative error of at most 0.018.
Values may be sent and summed in bfloat16 or wider, within the bound.
A program may use at most 128 MiB of HBM per device.

v0:
```python
import jax
import jax.numpy as jnp
from jax import lax
from jax.experimental import pallas as pl
from jax.experimental.pallas import tpu as pltpu
from jax.sharding import PartitionSpec as P

HEAD_DIM = 64
STATE = 128
HEADS_DEV = 8


epsilon = 1e-05


def scan_block(inputs, writes, readout, step_size, log_decay, resets, state, skips):
    segment = jnp.cumsum(resets)
    cumulative = jnp.cumsum(log_decay, axis=0)
    positions = jnp.arange(resets.shape[0])
    in_segment = (segment[:, None] == segment[None, :]) & (positions[:, None] >= positions[None, :])
    by_head = cumulative.T
    gap = by_head[:, :, None] - by_head[:, None, :]
    decayed = jnp.where(in_segment[None], jnp.exp(jnp.where(in_segment[None], gap, 0.0)), 0.0)
    f32 = jnp.float32
    scores = jnp.einsum("tn,sn->ts", readout, writes, preferred_element_type=f32)
    weights = scores[None] * decayed * step_size.T[:, None, :]
    output = jnp.einsum("hts,shp->thp", weights, inputs.astype(f32))
    carry_ok = (segment == 0).astype(f32)
    carried = jnp.einsum("tn,hpn->thp", readout.astype(f32), state)
    output = output + carry_ok[:, None, None] * jnp.exp(cumulative)[:, :, None] * carried
    last_seg = segment[-1]
    tail = (
        (segment == last_seg).astype(f32)[:, None]
        * jnp.exp(cumulative[-1][None, :] - cumulative)
        * step_size
    )
    fresh = jnp.einsum("shp,sn->hpn", tail[:, :, None] * inputs.astype(f32), writes.astype(f32))
    kept = (last_seg == 0).astype(f32) * jnp.exp(cumulative[-1])[:, None, None] * state
    output = output + skips[None, :, None] * inputs.astype(f32)
    return (output, fresh + kept)


CHUNKS = 2


MESH = pl.DeviceIdType.MESH


def greet(peers):
    barrier = pltpu.get_barrier_semaphore()
    for peer in peers:
        pl.semaphore_signal(barrier, inc=1, device_id=peer, device_id_type=MESH)
    pl.semaphore_wait(barrier, len(peers))


def remote_call(kernel, out_shape, operands, n_sems, collective_id):
    anywhere = pl.BlockSpec(memory_space=pl.ANY)
    sems = [pltpu.SemaphoreType.DMA((n_sems,)), pltpu.SemaphoreType.DMA((n_sems,))]
    return pl.pallas_call(
        kernel,
        out_shape=out_shape,
        in_specs=[anywhere] * len(operands),
        out_specs=[anywhere] * len(out_shape),
        scratch_shapes=sems,
        compiler_params=pltpu.CompilerParams(collective_id=collective_id, has_side_effects=True),
    )(*operands)


def send_all(jobs, collective_id):
    sizes = [lax.axis_size(axis) for _, axis, _ in jobs]
    operands = [array for array, _, _ in jobs]
    out_shape = []
    for (array, _, spread), n in zip(jobs, sizes):
        block = array.shape if spread else array.shape[1:]
        out_shape.append(jax.ShapeDtypeStruct((n - 1,) + block, array.dtype))
    axes = sorted({axis for _, axis, _ in jobs})
    n_sems = sum(n - 1 for n in sizes)

    def kernel(*refs):
        sources, targets = refs[: len(jobs)], refs[len(jobs) : 2 * len(jobs)]
        send_sem, recv_sem = refs[2 * len(jobs) :]
        peers = []
        for axis in axes:
            n = lax.axis_size(axis)
            peers += [{axis: lax.rem(lax.axis_index(axis) + k, n)} for k in range(1, n)]
        greet(peers)
        copies = []
        for (_, axis, spread), n, source, target in zip(jobs, sizes, sources, targets):
            for k in range(1, n):
                copy = pltpu.make_async_remote_copy(
                    src_ref=source if spread else source.at[k],
                    dst_ref=target.at[k - 1],
                    send_sem=send_sem.at[len(copies)],
                    recv_sem=recv_sem.at[len(copies)],
                    device_id={axis: lax.rem(lax.axis_index(axis) + k, n)},
                    device_id_type=MESH,
                )
                copy.start()
                copies.append(copy)
        for copy in copies:
            copy.wait()

    got = remote_call(kernel, out_shape, operands, n_sems, collective_id)
    results = []
    for (array, _, spread), n, out in zip(jobs, sizes, got):
        own = array if spread else array[0]
        results.append([own] + [out[k] for k in range(n - 1)])
    return results


def deliver(layers, collective_id):
    width, cores = lax.axis_size("tensor"), lax.axis_size("section")
    block = layers[0].shape[1:]
    out_shape = [jax.ShapeDtypeStruct((cores * width,) + block, layers[0].dtype)]

    def kernel(*refs):
        sources, (target, send_sem, recv_sem, local_sem) = refs[:cores], refs[cores:]
        core, lane = lax.axis_index("section"), lax.axis_index("tensor")

        def device(hop, k):
            return {
                "section": lax.rem(core + hop, cores), "tensor": lax.rem(lane + k, width)
            }

        pairs = [(h, k) for h in range(cores) for k in range(width) if h + k > 0]
        greet([device(h, k) for h, k in pairs])

        def send(layer, hop, k):
            return pltpu.make_async_remote_copy(
                src_ref=sources[layer].at[k],
                dst_ref=target.at[hop * width + k],
                send_sem=send_sem.at[hop * width + k],
                recv_sem=recv_sem.at[hop * width + k],
                device_id=device(hop, k),
                device_id_type=MESH,
            )

        for layer in range(cores):
            for hop in range(cores):
                @pl.when(lax.rem(core + hop, cores) == layer)
                def _():
                    for k in range(width):
                        if hop + k > 0:
                            send(layer, hop, k).start()
                        else:
                            pltpu.make_async_copy(
                                sources[layer].at[0], target.at[0], local_sem
                            ).start()
        for hop, k in pairs:
            send(0, hop, k).wait()
        pltpu.make_async_copy(sources[0].at[0], target.at[0], local_sem).wait()

    anywhere = pl.BlockSpec(memory_space=pl.ANY)
    sems = pltpu.SemaphoreType.DMA((cores * width,))
    out = pl.pallas_call(
        kernel,
        out_shape=out_shape,
        in_specs=[anywhere] * cores,
        out_specs=[anywhere],
        scratch_shapes=[sems, sems, pltpu.SemaphoreType.DMA],
        compiler_params=pltpu.CompilerParams(collective_id=collective_id, has_side_effects=True),
    )(*layers)[0]
    return out.reshape((cores, width) + block)


def shift(block, axis, distance):
    n = lax.axis_size(axis)
    return lax.ppermute(block, axis, [(i, (i + distance) % n) for i in range(n)])


def exchange(blocks, axis):
    return [b if k == 0 else shift(b, axis, k) for k, b in enumerate(blocks)]


def turned(stack, start):
    n = stack.shape[0]
    return lax.dynamic_slice_in_dim(jnp.concatenate([stack, stack], axis=0), start, n, axis=0)


def in_order(stack, me):
    n = stack.shape[0]
    return turned(stack[::-1], n - 1 - me)


def per_device(
    tokens, dest_slot, doc_reset, norm_gain, w_in, w_step, step_bias, a_log, d_skip, out_gain, w_out
):
    f32, bf16 = jnp.float32, jnp.bfloat16
    groups = lax.axis_size("dp")
    width = lax.axis_size("tensor")
    cores = lax.axis_size("section")
    group, lane, core = lax.axis_index("dp"), lax.axis_index("tensor"), lax.axis_index("section")
    row_count, feat_local = tokens.shape
    feats = feat_local * width
    depth = w_in.shape[1]
    head_cols = HEADS_DEV * HEAD_DIM
    half = row_count // cores
    src_few = half // width
    few = half // (CHUNKS * width)
    part = few * width

    w_in = lax.all_gather(w_in, "section", axis=0, tiled=True)
    w_out = lax.all_gather(w_out, "section", axis=0, tiled=True)
    step_own = lax.dynamic_slice_in_dim(w_step[0], group * depth, depth, axis=0)
    small = [norm_gain[0], step_bias[0], a_log[0], d_skip[0], out_gain[0]]
    joined = jnp.concatenate(small)[None]

    mine = lax.dynamic_slice_in_dim(tokens, core * half, half, axis=0)
    mine = turned(mine.reshape(width, src_few, feat_local), lane)
    jobs = [
        (mine, "tensor", False), (dest_slot[None], "dp", True),
        (joined, "section", True), (step_own, "section", True),
    ]
    mine, slots, joined, steps = send_all(jobs, 0)

    def by_layer(pair):
        return [jnp.where(core == layer, pair[0], pair[1]) for layer in range(cores)]

    w_step, joined = by_layer(steps), by_layer(joined)
    params, at = [], 0
    for piece in small:
        params.append([j[0, at : at + piece.shape[0]] for j in joined])
        at += piece.shape[0]
    norm_gain, step_bias, a_log, d_skip, out_gain = params

    mine = in_order(jnp.stack(mine), lane)
    mine = mine.transpose(1, 0, 2).reshape(src_few, groups, depth).transpose(1, 0, 2)
    (mine,) = send_all([(turned(mine, group), "dp", False)], 1)
    (parts,) = send_all([(jnp.stack(mine), "tensor", True)], 2)
    (pool,) = send_all([(jnp.stack(parts), "section", True)], 3)
    pool = jnp.stack(pool).reshape(-1, depth)

    slots = in_order(jnp.stack(slots), group).reshape(-1)
    wanted_group = lax.rem(group + jnp.arange(groups), groups)
    wanted = (
        wanted_group[None, :, None] * row_count
        + jnp.arange(CHUNKS)[:, None, None] * (cores * part)
        + core * part
        + jnp.arange(part)[None, None, :]
    ).reshape(-1)
    everyrow = jnp.arange(slots.shape[0], dtype=jnp.int32)
    source_of = jnp.sum(
        jnp.where(slots[None, :] == wanted[:, None], everyrow[None, :], 0), axis=1
    )
    src_group, inner = source_of // row_count, source_of % row_count
    src_core, inner = inner // half, inner % half
    src_lane, inner = inner // src_few, inner % src_few
    place = (core - src_core) % cores * width + (lane - src_lane) % width
    place = (place * groups + (group - src_group) % groups) * src_few + inner
    first = pool[place].reshape(CHUNKS, groups, part, depth)
    gain_own = lax.dynamic_slice_in_dim(norm_gain[0], group * depth, depth)

    def project(rows, layer):
        flat = rows.reshape(groups * part, depth)
        proj = jnp.dot(flat, w_in[layer], preferred_element_type=f32).astype(bf16)
        pre = jnp.dot(flat, w_step[layer], preferred_element_type=f32)
        return proj.reshape(groups, part, -1), pre.reshape(groups, part, -1)

    def packed(proj, side):
        high = lax.reduce_precision(side, 8, 7)
        low = lax.reduce_precision(side - high, 8, 7)
        return jnp.concatenate([proj, high.astype(bf16), low.astype(bf16)], axis=-1)

    def unpacked(total):
        cols = w_in.shape[-1]
        extra = (total.shape[-1] - cols) // 2
        return total[:, :cols], total[:, cols : cols + extra] + total[:, cols + extra :]

    def added(blocks):
        return sum(b.astype(f32) for b in blocks)

    def mix(proj, pre, resets, state, layer):
        proj = lax.all_gather(proj, "section", axis=0, tiled=True)
        pre = lax.all_gather(pre, "section", axis=0, tiled=True)
        count = proj.shape[0]
        step_size = jax.nn.softplus(pre + step_bias[layer])
        log_decay = -jnp.exp(a_log[layer]) * step_size
        mixed, state = scan_block(
            proj[:, head_cols : 2 * head_cols].reshape(count, HEADS_DEV, HEAD_DIM),
            proj[:, 2 * head_cols : 2 * head_cols + STATE],
            proj[:, 2 * head_cols + STATE :],
            step_size,
            log_decay,
            resets,
            state,
            d_skip[layer],
        )
        mixed = mixed.reshape(count, head_cols)
        mixed = lax.dynamic_slice_in_dim(mixed, core * part, part, axis=0)
        gate = lax.dynamic_slice_in_dim(proj[:, :head_cols], core * part, part, axis=0).astype(f32)
        gated = mixed * jax.nn.silu(gate)
        meansq_out = jnp.mean(gated * gated, axis=-1, keepdims=True)
        normed = (gated * lax.rsqrt(meansq_out + epsilon) * out_gain[layer]).astype(bf16)
        normed = turned(normed.reshape(width, few, head_cols), lane).reshape(part, head_cols)
        partial_value = jnp.dot(normed, w_out[layer], preferred_element_type=f32).astype(bf16)
        blocks = partial_value.reshape(width, few, feats)
        return added(exchange([blocks[k] for k in range(width)], "tensor")), state

    resets = doc_reset.reshape(CHUNKS, -1)
    zero_state = jnp.zeros((HEADS_DEV, HEAD_DIM, STATE), f32)
    sent = []
    for c in range(CHUNKS):
        wide = first[c].astype(f32)
        squares = jnp.sum(wide * wide, axis=-1)
        proj, pre = project((wide * gain_own).astype(bf16), 0)
        side = jnp.concatenate([pre, squares[:, :, None]], axis=-1)
        kept = lax.dynamic_slice_in_dim(first[c], lane * few, few, axis=1)
        proj = packed(proj, side)
        proj = exchange([proj[k] for k in range(groups)], "dp")
        kept = exchange([kept[k] for k in range(groups)], "dp")
        sent.append((proj, kept))
    state = zero_state
    middle, outs = [], []
    for c in range(CHUNKS):
        proj, kept = sent[c]
        proj, side = unpacked(added(proj))
        scale = lax.rsqrt(side[:, HEADS_DEV:] / feats + epsilon)
        summed, state = mix(
            (proj * scale).astype(bf16), side[:, :HEADS_DEV] * scale, resets[c], state, 0
        )
        kept = in_order(jnp.stack(kept), group).transpose(1, 0, 2).reshape(few, feats)
        rows = (kept.astype(f32) + summed).astype(bf16)
        middle.append(rows)
        widened = rows.astype(f32)
        meansq = jnp.mean(widened * widened, axis=-1, keepdims=True)
        u = (widened * lax.rsqrt(meansq + epsilon) * norm_gain[1]).astype(bf16)
        u = turned(u.reshape(few, groups, depth).transpose(1, 0, 2), group)
        u = jnp.stack(exchange([u[k] for k in range(groups)], "dp"))
        u = jnp.stack(exchange([u] * width, "tensor"), axis=1)
        proj, pre = project(u, 1)
        back = [(groups - k) % groups for k in range(groups)]
        both = packed(proj, pre)
        sent[c] = exchange([both[k] for k in back], "dp")
    state = zero_state
    for c in range(CHUNKS):
        proj, pre = unpacked(added(sent[c]))
        proj = in_order(proj.astype(bf16).reshape(width, few, -1), lane).reshape(part, -1)
        pre = in_order(pre.reshape(width, few, -1), lane).reshape(part, -1)
        summed, state = mix(proj, pre, resets[c], state, 1)
        rows = (middle[c].astype(f32) + summed).astype(bf16)
        outs.append(rows)

    def for_lanes(rows):
        both = jnp.stack(rows).reshape(CHUNKS, few, width, feat_local).transpose(2, 0, 1, 3)
        return turned(both, lane)

    out = deliver([for_lanes(middle), for_lanes(outs)], 4)
    out = jnp.stack([in_order(out[hop], lane) for hop in range(cores)])
    out = in_order(out, core).transpose(2, 0, 1, 3, 4)
    return out.reshape(1, row_count, feat_local)


def solution(mesh):
    placed = (
        P("dp", "tensor"),
        P("dp"),
        P("dp"),
        P("section", None),
        P("section", "dp", "tensor"),
        P("section", None, "tensor"),
        P("section", "tensor"),
        P("section", "tensor"),
        P("section", "tensor"),
        P("section", "tensor"),
        P("section", "tensor", None),
    )
    return jax.shard_map(
        per_device,
        mesh=mesh,
        in_specs=placed,
        out_specs=P("section", "dp", "tensor"),
        check_vma=False,
    )
```

profile of v0, /device:TPU:1, one launch (start us, length us, event | category | flops | bytes accessed | tf_op | source)
XLA Modules:
  0.0 344.2 jit_solution(15433618635935113440)
XLA Ops:
  11.7 11.6 %shard_map.109 = (bf16[3,32,2048]{2,1,0:T(8,128)(2,1)}, s32[3,1,256]{2,1,0:T(1,128)}, f32[1,1,8728]{2,1,0:T(1,128)}, bf16[1,2048,8]{2,1,0:T(8,128)(2,1)}) custom-call(bf16[4,32,2048]{2,1,0:T(8,128)(2,1)} %copy-done.6, s32[1,256]{1,0:T(1,128)} %bitcast.394, f32[1,8728]{1,0:T(1,128)} %broadcast_in_dim.71.refs_2_, bf16[2048,8]{1,0:T(8,128)(2,1)} %bitcast.323), custom_call_target="tpu_custom_call" | custom-call | tf_op jit(solution)/shard_map/pallas_call | solution.py:59
  25.7 11.0 %shard_map.110 = bf16[3,32,2048]{2,1,0:T(8,128)(2,1)} custom-call(bf16[4,32,2048]{2,1,0:T(8,128)(2,1)} %fusion.36.refs_0_), custom_call_target="tpu_custom_call" | custom-call | tf_op jit(solution)/shard_map/pallas_call | solution.py:59
  37.6 1.9 fusion.211
  39.5 25.1 %shard_map.111 = bf16[3,4,32,2048]{3,2,1,0:T(8,128)(2,1)} custom-call(bf16[4,32,2048]{2,1,0:T(8,128)(2,1)} %get-tuple-element.62.refs_0_), custom_call_target="tpu_custom_call" | custom-call | tf_op jit(solution)/shard_map/pallas_call | solution.py:59
  64.6 3.1 fusion.214
  67.7 6.6 %shard_map.112 = bf16[1,4,4,32,2048]{4,3,2,1,0:T(8,128)(2,1)} custom-call(bf16[4,4,32,2048]{3,2,1,0:T(8,128)(2,1)} %get-tuple-element.26.refs_0_), custom_call_target="tpu_custom_call" | custom-call | tf_op jit(solution)/shard_map/pallas_call | solution.py:59
  75.2 4.0 %pad_maximum_fusion = bf16[2,4,4,32,2048]{4,3,2,1,0:T(8,128)(2,1)} fusion(bf16[1,4,4,32,2048]{4,3,2,1,0:T(8,128)(2,1)} %shard_map.112, bf16[1,4,4,32,2048]{4,3,2,1,0:T(8,128)(2,1)S(1)} %get-tuple-element.25), kind=kLoop, calls=%fused_computation.13 | loop fusion | flops 2097152 | bytes 8388608 | tf_op jit(solution)/shard_map/stack | solution.py:231
  79.2 7.1 %gather_fusion = bf16[512,2048]{1,0:T(8,128)(2,1)S(1)} fusion(bf16[1024,2048]{1,0:T(8,128)(2,1)} %bitcast.322, s32[1024]{0:T(1024)S(1)} %pad_clamp_fusion), kind=kCustom, calls=%fused_computation | custom fusion | bytes 4196352 | tf_op jit(solution)/shard_map/gather | solution.py:250
  86.4 1.5 fusion.215
  87.8 1.6 constant_dynamic-slice_fusion.4
  89.4 4.7 %collective-permute-start.11 = (bf16[16,2048]{1,0:T(8,128)(2,1)}, bf16[16,2048]{1,0:T(8,128)(2,1)}, u32[]{:S(2)}, u32[]{:S(2)}) collective-permute-start(bf16[16,2048]{1,0:T(8,128)(2,1)} %get-tuple-element.48), channel_id=1, source_target_pairs={{0,24},{8,0},{16,8},{24,16},{1,25},{9,1},{17,9},{25,17},{2,26},{10... | collective-permute-start | bytes 196616 | tf_op jit(solution)/shard_map/ppermute | solution.py:168
  94.5 1.6 constant_dynamic-slice_fusion
  96.1 3.0 collective-permute-start.2
  102.7 1.6 fusion.8
  105.5 1.7 fusion.43
  107.9 1.2 compare_convert_fusion.2
  111.2 1.7 fusion.45
  116.2 2.9 collective-permute-done
  121.0 4.9 %fusion.6 = bf16[256,1280]{1,0:T(8,128)(2,1)} fusion(bf16[256,2048]{1,0:T(8,128)(2,1)S(1)} %copy-done.5, bf16[2,2048,1280]{2,1,0:T(8,128)(2,1)} %all-gather.7.cloned.1.call-done), kind=kOutput, calls=%fused_computation.20 | convolution fusion | flops 1342504960 | bytes 6946816 | tf_op jit(solution)/shard_map/dot_general | solution.py:255
  129.5 4.0 %fusion.7 = bf16[256,1280]{1,0:T(8,128)(2,1)S(1)} fusion(bf16[256,2048]{1,0:T(8,128)(2,1)S(1)} %copy-done.4, bf16[2,2048,1280]{2,1,0:T(8,128)(2,1)} %all-gather.7.cloned.1.call-done), kind=kOutput, calls=%fused_computation.21 | convolution fusion | flops 1342504960 | bytes 6946816 | tf_op jit(solution)/shard_map/dot_general | solution.py:255
  135.2 2.1 collective-permute-start.14
  139.0 3.2 collective-permute-done.4
  143.8 15.4 %all_gather.31 = bf16[128,1280]{1,0:T(8,128)(2,1)S(1)} all-gather(bf16[64,1280]{1,0:T(8,128)(2,1)S(1)} %fusion.80), channel_id=1, replica_groups=mesh['dp'=4,'section'=2,'tensor'=4] {'section'}, dimensions={0}, use_global_device_ids=true | all-gather | bytes 491520 | tf_op jit(solution)/shard_map/all_gather | solution.py:273
  159.4 1.8 all-gather
  162.8 1.8 all-gather.1
  170.0 2.0 all_gather.34
  175.7 4.9 %convolution_convert_fusion.3 = bf16[64,8192]{1,0:T(8,128)(2,1)S(1)} fusion(bf16[64,512]{1,0:T(8,128)(2,1)S(1)} %bitcast.383, bf16[2,512,8192]{2,1,0:T(8,128)(2,1)} %all-gather.9.cloned.1.call-done), kind=kOutput, calls=%fused_computation.4 | convolution fusion | flops 537395200 | bytes 9502720 | tf_op jit(solution)/shard_map/dot_general | solution.py:295
  180.7 1.2 collective-permute-start.8
  182.7 5.0 %convolution_convert_fusion.2 = bf16[64,8192]{1,0:T(8,128)(2,1)S(1)} fusion(bf16[64,512]{1,0:T(8,128)(2,1)S(1)} %bitcast.382, bf16[2,512,8192]{2,1,0:T(8,128)(2,1)} %all-gather.9.cloned.1.call-done), kind=kOutput, calls=%fused_computation.3 | convolution fusion | flops 537395200 | bytes 9502720 | tf_op jit(solution)/shard_map/dot_general | solution.py:295
  187.8 2.4 collective-permute-start.17
  191.0 3.0 collective-permute-done.6
  194.3 5.3 %collective-permute-done.17 = bf16[16,8192]{1,0:T(8,128)(2,1)S(1)} collective-permute-done((bf16[16,8192]{1,0:T(8,128)(2,1)S(1)}, bf16[16,8192]{1,0:T(8,128)(2,1)S(1)}, u32[]{:S(2)}, u32[]{:S(2)}) %collective-permute-start.17) | collective-permute-done | bytes 262176 | tf_op jit(solution)/shard_map/ppermute | solution.py:168
  199.6 1.7 collective-permute-done.16
  201.3 4.0 %collective-permute-done.15 = bf16[16,8192]{1,0:T(8,128)(2,1)S(1)} collective-permute-done((bf16[16,8192]{1,0:T(8,128)(2,1)S(1)}, bf16[16,8192]{1,0:T(8,128)(2,1)S(1)}, u32[]{:S(2)}, u32[]{:S(2)}) %collective-permute-start.15) | collective-permute-done | bytes 262176 | tf_op jit(solution)/shard_map/ppermute | solution.py:168
  206.0 1.8 collective-permute-start.19
  207.8 1.4 collective-permute-start.18
  209.8 1.9 collective-permute-start.32
  213.0 1.8 collective-permute-start.23
  214.8 2.1 collective-permute-start.22
  217.7 1.3 collective-permute-done.31
  219.9 2.4 collective-permute-start.35
  222.3 1.6 collective-permute-start.34
  224.1 1.5 collective-permute-done.21
  226.6 4.8 %fusion.4 = bf16[256,1280]{1,0:T(8,128)(2,1)} fusion(bf16[256,2048]{1,0:T(8,128)(2,1)S(1)} %bitcast.327, bf16[2,2048,1280]{2,1,0:T(8,128)(2,1)} %all-gather.7.cloned.1.call-done), kind=kOutput, calls=%fused_computation.18 | convolution fusion | flops 1342504960 | bytes 6946816 | tf_op jit(solution)/shard_map/dot_general | solution.py:255
  233.5 2.2 collective-permute-start.26
  236.9 1.3 pad_maximum_fusion.3
  239.1 4.8 %fusion.5 = bf16[256,1280]{1,0:T(8,128)(2,1)} fusion(bf16[256,2048]{1,0:T(8,128)(2,1)S(1)} %bitcast.325, bf16[2,2048,1280]{2,1,0:T(8,128)(2,1)} %all-gather.7.cloned.1.call-done), kind=kOutput, calls=%fused_computation.19 | convolution fusion | flops 1342504960 | bytes 6946816 | tf_op jit(solution)/shard_map/dot_general | solution.py:255
  245.3 2.2 collective-permute-start.38
  249.4 11.2 %all-gather.2 = f32[2,64,8]{1,2,0:T(8,128)S(1)} all-gather(f32[1,64,8]{1,2,0:T(8,128)S(1)} %reshape.1086), channel_id=1, replica_groups=mesh['dp'=4,'section'=2,'tensor'=4] {'section'}, dimensions={0}, use_global_device_ids=true | all-gather | bytes 6144 | tf_op jit(solution)/shard_map/all_gather | solution.py:274
  260.6 6.7 %collective-permute-done.37 = bf16[64,1296]{1,0:T(8,128)(2,1)S(1)} collective-permute-done((bf16[64,1296]{1,0:T(8,128)(2,1)S(1)}, bf16[64,1296]{1,0:T(8,128)(2,1)S(1)}, u32[]{:S(2)}, u32[]{:S(2)}) %collective-permute-start.37) | collective-permute-done | bytes 165920 | tf_op jit(solution)/shard_map/ppermute | solution.py:168
  268.6 3.4 all-gather.3
  272.7 2.0 all_gather.36
  275.1 2.0 all_gather.38
  280.7 5.0 %convolution_convert_fusion = bf16[64,8192]{1,0:T(8,128)(2,1)S(1)} fusion(bf16[64,512]{1,0:T(8,128)(2,1)S(1)} %bitcast.385, bf16[2,512,8192]{2,1,0:T(8,128)(2,1)} %all-gather.9.cloned.1.call-done), kind=kOutput, calls=%fused_computation.1 | convolution fusion | flops 537395200 | bytes 9502720 | tf_op jit(solution)/shard_map/dot_general | solution.py:295
  285.7 5.6 %collective-permute-start.41 = (bf16[16,8192]{1,0:T(8,128)(2,1)S(1)}, bf16[16,8192]{1,0:T(8,128)(2,1)S(1)}, u32[]{:S(2)}, u32[]{:S(2)}) collective-permute-start(bf16[16,8192]{1,0:T(8,128)(2,1)S(1)} %get-tuple-element.33), channel_id=1, source_target_pairs={{0,3},{1,0},{2,1},{3,2},{4,7},{5,4},{6,5},{7,6},{8,11},{9,8},{10,9... | collective-permute-start | bytes 786440 | tf_op jit(solution)/shard_map/ppermute | solution.py:168
  291.7 5.0 %convolution_convert_fusion.1 = bf16[64,8192]{1,0:T(8,128)(2,1)S(1)} fusion(bf16[64,512]{1,0:T(8,128)(2,1)S(1)} %bitcast.384, bf16[2,512,8192]{2,1,0:T(8,128)(2,1)} %all-gather.9.cloned.1.call-done), kind=kOutput, calls=%fused_computation.2 | convolution fusion | flops 537395200 | bytes 9502720 | tf_op jit(solution)/shard_map/dot_general | solution.py:295
  297.6 2.0 collective-permute-start.29
  299.6 1.5 collective-permute-start.28
  301.0 3.0 collective-permute-done.40
  304.5 3.6 %collective-permute-done.29 = bf16[16,8192]{1,0:T(8,128)(2,1)S(1)} collective-permute-done((bf16[16,8192]{1,0:T(8,128)(2,1)}, bf16[16,8192]{1,0:T(8,128)(2,1)S(1)}, u32[]{:S(2)}, u32[]{:S(2)}) %collective-permute-start.29) | collective-permute-done | bytes 262176 | tf_op jit(solution)/shard_map/ppermute | solution.py:168
  308.1 7.3 %collective-permute-done.28 = bf16[16,8192]{1,0:T(8,128)(2,1)S(1)} collective-permute-done((bf16[16,8192]{1,0:T(8,128)(2,1)}, bf16[16,8192]{1,0:T(8,128)(2,1)S(1)}, u32[]{:S(2)}, u32[]{:S(2)}) %collective-permute-start.28) | collective-permute-done | bytes 262176 | tf_op jit(solution)/shard_map/ppermute | solution.py:168
  317.0 1.4 fusion.34
  318.3 15.6 %shard_map.113 = bf16[8,2,16,2048]{3,2,1,0:T(8,128)(2,1)} custom-call(bf16[4,2,16,2048]{3,2,1,0:T(8,128)(2,1)} %get-tuple-element.120.refs_0_, bf16[4,2,16,2048]{3,2,1,0:T(8,128)(2,1)} %get-tuple-element.119.refs_1_), custom_call_target="tpu_custom_call" | custom-call | tf_op jit(solution)/shard_map/pallas_call | solution.py:155
  333.9 1.3 fusion.216
  (346 shorter events, 66.2 us)
Async XLA Ops:
  6.5 114.5 %all-gather.7.cloned.1.call-start = ((), (), s32[]{:S(2)}) async-start(), calls=%async_computation | async-start | bytes 15728640 | tf_op jit(solution)/shard_map/all_gather | solution.py:202
  7.3 168.4 %all-gather.9.cloned.1.call-start = ((), (), s32[]{:S(2)}) async-start(), calls=%async_computation.1 | async-start | bytes 25165824 | tf_op jit(solution)/shard_map/all_gather | solution.py:203
  64.6 9.7 %copy-start.22 = (s32[256]{0:T(256)S(1)}, s32[256]{0:T(256)}, u32[]{:S(2)}) copy-start(s32[256]{0:T(256)} %param.12) | copy-start | bytes 3076
  64.6 9.7 %copy-start.23 = (s32[3,1,256]{2,1,0:T(1,128)S(1)}, s32[3,1,256]{2,1,0:T(1,128)}, u32[]{:S(2)}) copy-start(s32[3,1,256]{2,1,0:T(1,128)} %get-tuple-element.10) | copy-start | bytes 9220
  86.3 13.4 %copy-start.13 = (f32[1,1,8728]{2,1,0:T(1,128)S(1)}, f32[1,1,8728]{2,1,0:T(1,128)}, u32[]{:S(2)}) copy-start(f32[1,1,8728]{2,1,0:T(1,128)} %get-tuple-element.11) | copy-start | bytes 104740
  86.3 14.1 %copy-start.29 = (s32[256]{0:T(256)S(1)}, s32[256]{0:T(256)}, u32[]{:S(2)}) copy-start(s32[256]{0:T(256)} %param.13) | copy-start | bytes 3076
  86.3 19.2 %copy-start.2 = (bf16[1,2048,8]{2,1,0:T(8,128)(2,1)S(1)}, bf16[1,2048,8]{2,1,0:T(8,128)(2,1)}, u32[]{:S(2)}) copy-start(bf16[1,2048,8]{2,1,0:T(8,128)(2,1)} %copy.371) | copy-start | bytes 98308
  86.4 19.2 %copy-start.3 = (bf16[1,2048,8]{2,1,0:T(8,128)(2,1)S(1)}, bf16[1,2048,8]{2,1,0:T(8,128)(2,1)}, u32[]{:S(2)}) copy-start(bf16[1,2048,8]{2,1,0:T(8,128)(2,1)} %get-tuple-element.12) | copy-start | bytes 98308
  89.4 24.7 %collective-permute-start.11 = (bf16[16,2048]{1,0:T(8,128)(2,1)}, bf16[16,2048]{1,0:T(8,128)(2,1)}, u32[]{:S(2)}, u32[]{:S(2)}) collective-permute-start(bf16[16,2048]{1,0:T(8,128)(2,1)} %get-tuple-element.48), channel_id=1, source_target_pairs={{0,24},{8,0},{16,8},{24,16},{1,25},{9,1},{17,9},{25,17},{2,26},{10... | collective-permute-start | bytes 196616 | tf_op jit(solution)/shard_map/ppermute | solution.py:168
  94.2 20.0 %collective-permute-start.10 = (bf16[16,2048]{1,0:T(8,128)(2,1)}, bf16[16,2048]{1,0:T(8,128)(2,1)}, u32[]{:S(2)}, u32[]{:S(2)}) collective-permute-start(bf16[16,2048]{1,0:T(8,128)(2,1)} %get-tuple-element.46), channel_id=1, source_target_pairs={{0,16},{8,24},{16,0},{24,8},{1,17},{9,25},{17,1},{25,9},{2,18},{10... | collective-permute-start | bytes 196616 | tf_op jit(solution)/shard_map/ppermute | solution.py:168
  94.2 20.0 %collective-permute-start.9 = (bf16[16,2048]{1,0:T(8,128)(2,1)}, bf16[16,2048]{1,0:T(8,128)(2,1)}, u32[]{:S(2)}, u32[]{:S(2)}) collective-permute-start(bf16[16,2048]{1,0:T(8,128)(2,1)} %get-tuple-element.47), channel_id=1, source_target_pairs={{0,8},{8,16},{16,24},{24,0},{1,9},{9,17},{17,25},{25,1},{2,10},{10... | collective-permute-start | bytes 196616 | tf_op jit(solution)/shard_map/ppermute | solution.py:168
  96.1 20.1 %collective-permute-start.2 = (bf16[16,2048]{1,0:T(8,128)(2,1)}, bf16[16,2048]{1,0:T(8,128)(2,1)}, u32[]{:S(2)}, u32[]{:S(2)}) collective-permute-start(bf16[16,2048]{1,0:T(8,128)(2,1)} %get-tuple-element.41), channel_id=1, source_target_pairs={{0,24},{8,0},{16,8},{24,16},{1,25},{9,1},{17,9},{25,17},{2,26},{10... | collective-permute-start | bytes 196616 | tf_op jit(solution)/shard_map/ppermute | solution.py:168
  99.1 17.1 %collective-permute-start.1 = (bf16[16,2048]{1,0:T(8,128)(2,1)}, bf16[16,2048]{1,0:T(8,128)(2,1)}, u32[]{:S(2)}, u32[]{:S(2)}) collective-permute-start(bf16[16,2048]{1,0:T(8,128)(2,1)} %get-tuple-element.39), channel_id=1, source_target_pairs={{0,16},{8,24},{16,0},{24,8},{1,17},{9,25},{17,1},{25,9},{2,18},{10... | collective-permute-start | bytes 196616 | tf_op jit(solution)/shard_map/ppermute | solution.py:168
  104.3 9.9 %copy-start.12 = (bf16[16,2048]{1,0:T(8,128)(2,1)S(1)}, bf16[16,2048]{1,0:T(8,128)(2,1)}, u32[]{:S(2)}) copy-start(bf16[16,2048]{1,0:T(8,128)(2,1)} %get-tuple-element.40) | copy-start | bytes 196612
  107.3 13.8 %copy-start.5 = (bf16[256,2048]{1,0:T(8,128)(2,1)S(1)}, bf16[256,2048]{1,0:T(8,128)(2,1)}, u32[]{:S(2)}) copy-start(bf16[256,2048]{1,0:T(8,128)(2,1)} %get-tuple-element.19) | copy-start | bytes 3145732
  114.2 4.9 %collective-permute-start = (bf16[16,2048]{1,0:T(8,128)(2,1)S(1)}, bf16[16,2048]{1,0:T(8,128)(2,1)S(1)}, u32[]{:S(2)}, u32[]{:S(2)}) collective-permute-start(bf16[16,2048]{1,0:T(8,128)(2,1)S(1)} %copy-done.12), channel_id=1, source_target_pairs={{0,8},{8,16},{16,24},{24,0},{1,9},{9,17},{17,25},{25,1},{2,10},{10... | collective-permute-start | bytes 196616 | tf_op jit(solution)/shard_map/ppermute | solution.py:168
  121.0 8.4 %copy-start.4 = (bf16[256,2048]{1,0:T(8,128)(2,1)S(1)}, bf16[256,2048]{1,0:T(8,128)(2,1)}, u32[]{:S(2)}) copy-start(bf16[256,2048]{1,0:T(8,128)(2,1)} %get-tuple-element.20) | copy-start | bytes 3145732
  128.0 9.9 %collective-permute-start.5 = (bf16[64,1298]{1,0:T(8,128)(2,1)}, bf16[64,1298]{1,0:T(8,128)(2,1)}, u32[]{:S(2)}, u32[]{:S(2)}) collective-permute-start(bf16[64,1298]{1,0:T(8,128)(2,1)} %get-tuple-element.56), channel_id=1, source_target_pairs={{0,24},{8,0},{16,8},{24,16},{1,25},{9,1},{17,9},{25,17},{2,26},{10... | collective-permute-start | bytes 498440 | tf_op jit(solution)/shard_map/ppermute | solution.py:168
  128.3 13.9 %collective-permute-start.4 = (bf16[64,1298]{1,0:T(8,128)(2,1)}, bf16[64,1298]{1,0:T(8,128)(2,1)}, u32[]{:S(2)}, u32[]{:S(2)}) collective-permute-start(bf16[64,1298]{1,0:T(8,128)(2,1)} %get-tuple-element.57), channel_id=1, source_target_pairs={{0,16},{8,24},{16,0},{24,8},{1,17},{9,25},{17,1},{25,9},{2,18},{10... | collective-permute-start | bytes 498440 | tf_op jit(solution)/shard_map/ppermute | solution.py:168
  128.3 13.9 %collective-permute-start.3 = (bf16[64,1298]{1,0:T(8,128)(2,1)}, bf16[64,1298]{1,0:T(8,128)(2,1)}, u32[]{:S(2)}, u32[]{:S(2)}) collective-permute-start(bf16[64,1298]{1,0:T(8,128)(2,1)} %get-tuple-element.55), channel_id=1, source_target_pairs={{0,8},{8,16},{16,24},{24,0},{1,9},{9,17},{17,25},{25,1},{2,10},{10... | collective-permute-start | bytes 498440 | tf_op jit(solution)/shard_map/ppermute | solution.py:168
  135.2 26.2 %collective-permute-start.14 = (bf16[64,1298]{1,0:T(8,128)(2,1)}, bf16[64,1298]{1,0:T(8,128)(2,1)S(1)}, u32[]{:S(2)}, u32[]{:S(2)}) collective-permute-start(bf16[64,1298]{1,0:T(8,128)(2,1)} %get-tuple-element.59), channel_id=1, source_target_pairs={{0,24},{8,0},{16,8},{24,16},{1,25},{9,1},{17,9},{25,17},{2,26},{10... | collective-permute-start | bytes 498440 | tf_op jit(solution)/shard_map/ppermute | solution.py:168
  137.3 24.0 %collective-permute-start.13 = (bf16[64,1298]{1,0:T(8,128)(2,1)S(1)}, bf16[64,1298]{1,0:T(8,128)(2,1)S(1)}, u32[]{:S(2)}, u32[]{:S(2)}) collective-permute-start(bf16[64,1298]{1,0:T(8,128)(2,1)S(1)} %get-tuple-element.60), channel_id=1, source_target_pairs={{0,16},{8,24},{16,0},{24,8},{1,17},{9,25},{17,1},{25,9},{2,18},{10... | collective-permute-start | bytes 498440 | tf_op jit(solution)/shard_map/ppermute | solution.py:168
  137.9 23.5 %collective-permute-start.12 = (bf16[64,1298]{1,0:T(8,128)(2,1)S(1)}, bf16[64,1298]{1,0:T(8,128)(2,1)}, u32[]{:S(2)}, u32[]{:S(2)}) collective-permute-start(bf16[64,1298]{1,0:T(8,128)(2,1)S(1)} %get-tuple-element.58), channel_id=1, source_target_pairs={{0,8},{8,16},{16,24},{24,0},{1,9},{9,17},{17,25},{25,1},{2,10},{10... | collective-permute-start | bytes 498440 | tf_op jit(solution)/shard_map/ppermute | solution.py:168
  180.7 10.2 %collective-permute-start.8 = (bf16[16,8192]{1,0:T(8,128)(2,1)S(1)}, bf16[16,8192]{1,0:T(8,128)(2,1)S(1)}, u32[]{:S(2)}, u32[]{:S(2)}) collective-permute-start(bf16[16,8192]{1,0:T(8,128)(2,1)S(1)} %get-tuple-element.36), channel_id=1, source_target_pairs={{0,3},{1,0},{2,1},{3,2},{4,7},{5,4},{6,5},{7,6},{8,11},{9,8},{10,9... | collective-permute-start | bytes 786440 | tf_op jit(solution)/shard_map/ppermute | solution.py:168
  182.0 9.0 %collective-permute-start.7 = (bf16[16,8192]{1,0:T(8,128)(2,1)S(1)}, bf16[16,8192]{1,0:T(8,128)(2,1)S(1)}, u32[]{:S(2)}, u32[]{:S(2)}) collective-permute-start(bf16[16,8192]{1,0:T(8,128)(2,1)S(1)} %get-tuple-element.37), channel_id=1, source_target_pairs={{0,2},{1,3},{2,0},{3,1},{4,6},{5,7},{6,4},{7,5},{8,10},{9,11},{10,... | collective-permute-start | bytes 786440 | tf_op jit(solution)/shard_map/ppermute | solution.py:168
  182.7 11.3 %collective-permute-start.6 = (bf16[16,8192]{1,0:T(8,128)(2,1)S(1)}, bf16[16,8192]{1,0:T(8,128)(2,1)S(1)}, u32[]{:S(2)}, u32[]{:S(2)}) collective-permute-start(bf16[16,8192]{1,0:T(8,128)(2,1)S(1)} %get-tuple-element.35), channel_id=1, source_target_pairs={{0,1},{1,2},{2,3},{3,0},{4,5},{5,6},{6,7},{7,4},{8,9},{9,10},{10,1... | collective-permute-start | bytes 786440 | tf_op jit(solution)/shard_map/ppermute | solution.py:168
  182.7 11.3 %copy-start.9 = (f32[4,2,8,2048]{3,2,0,1:T(8,128)S(1)}, f32[4,2,8,2048]{3,2,0,1:T(8,128)}, u32[]{:S(2)}) copy-start(f32[4,2,8,2048]{3,2,0,1:T(8,128)} %copy.378) | copy-start | bytes 1572868
  182.7 22.6 %copy-start.8 = (f32[4,2,8,2048]{3,2,0,1:T(8,128)S(1)}, f32[4,2,8,2048]{3,2,0,1:T(8,128)}, u32[]{:S(2)}) copy-start(f32[4,2,8,2048]{3,2,0,1:T(8,128)} %copy.379) | copy-start | bytes 1572868
  187.8 17.8 %copy-start.10 = (f32[1,8192]{1,0:T(1,128)S(1)}, f32[1,8192]{1,0:T(1,128)}, u32[]{:S(2)}) copy-start(f32[1,8192]{1,0:T(1,128)} %slice.521) | copy-start | bytes 98308
  187.8 11.8 %collective-permute-start.17 = (bf16[16,8192]{1,0:T(8,128)(2,1)S(1)}, bf16[16,8192]{1,0:T(8,128)(2,1)S(1)}, u32[]{:S(2)}, u32[]{:S(2)}) collective-permute-start(bf16[16,8192]{1,0:T(8,128)(2,1)S(1)} %get-tuple-element.43), channel_id=1, source_target_pairs={{0,3},{1,0},{2,1},{3,2},{4,7},{5,4},{6,5},{7,6},{8,11},{9,8},{10,9... | collective-permute-start | bytes 786440 | tf_op jit(solution)/shard_map/ppermute | solution.py:168
  190.2 11.0 %collective-permute-start.16 = (bf16[16,8192]{1,0:T(8,128)(2,1)S(1)}, bf16[16,8192]{1,0:T(8,128)(2,1)S(1)}, u32[]{:S(2)}, u32[]{:S(2)}) collective-permute-start(bf16[16,8192]{1,0:T(8,128)(2,1)S(1)} %get-tuple-element.44), channel_id=1, source_target_pairs={{0,2},{1,3},{2,0},{3,1},{4,6},{5,7},{6,4},{7,5},{8,10},{9,11},{10,... | collective-permute-start | bytes 786440 | tf_op jit(solution)/shard_map/ppermute | solution.py:168
  191.0 14.3 %collective-permute-start.15 = (bf16[16,8192]{1,0:T(8,128)(2,1)S(1)}, bf16[16,8192]{1,0:T(8,128)(2,1)S(1)}, u32[]{:S(2)}, u32[]{:S(2)}) collective-permute-start(bf16[16,8192]{1,0:T(8,128)(2,1)S(1)} %get-tuple-element.42), channel_id=1, source_target_pairs={{0,1},{1,2},{2,3},{3,0},{4,5},{5,6},{6,7},{7,4},{8,9},{9,10},{10,1... | collective-permute-start | bytes 786440 | tf_op jit(solution)/shard_map/ppermute | solution.py:168
  206.0 6.1 %collective-permute-start.20 = (bf16[16,2048]{1,0:T(8,128)(2,1)S(1)}, bf16[16,2048]{1,0:T(8,128)(2,1)S(1)}, u32[]{:S(2)}, u32[]{:S(2)}) collective-permute-start(bf16[16,2048]{1,0:T(8,128)(2,1)S(1)} %get-tuple-element.76), channel_id=1, source_target_pairs={{0,24},{8,0},{16,8},{24,16},{1,25},{9,1},{17,9},{25,17},{2,26},{10... | collective-permute-start | bytes 196616 | tf_op jit(solution)/shard_map/ppermute | solution.py:168
  206.0 6.4 %collective-permute-start.19 = (bf16[16,2048]{1,0:T(8,128)(2,1)S(1)}, bf16[16,2048]{1,0:T(8,128)(2,1)S(1)}, u32[]{:S(2)}, u32[]{:S(2)}) collective-permute-start(bf16[16,2048]{1,0:T(8,128)(2,1)S(1)} %get-tuple-element.74), channel_id=1, source_target_pairs={{0,16},{8,24},{16,0},{24,8},{1,17},{9,25},{17,1},{25,9},{2,18},{10... | collective-permute-start | bytes 196616 | tf_op jit(solution)/shard_map/ppermute | solution.py:168
  207.8 5.1 %collective-permute-start.18 = (bf16[16,2048]{1,0:T(8,128)(2,1)S(1)}, bf16[16,2048]{1,0:T(8,128)(2,1)S(1)}, u32[]{:S(2)}, u32[]{:S(2)}) collective-permute-start(bf16[16,2048]{1,0:T(8,128)(2,1)S(1)} %get-tuple-element.75), channel_id=1, source_target_pairs={{0,8},{8,16},{16,24},{24,0},{1,9},{9,17},{17,25},{25,1},{2,10},{10... | collective-permute-start | bytes 196616 | tf_op jit(solution)/shard_map/ppermute | solution.py:168
  209.8 7.1 %collective-permute-start.32 = (bf16[16,2048]{1,0:T(8,128)(2,1)S(1)}, bf16[16,2048]{1,0:T(8,128)(2,1)S(1)}, u32[]{:S(2)}, u32[]{:S(2)}) collective-permute-start(bf16[16,2048]{1,0:T(8,128)(2,1)S(1)} %get-tuple-element.82), channel_id=1, source_target_pairs={{0,24},{8,0},{16,8},{24,16},{1,25},{9,1},{17,9},{25,17},{2,26},{10... | collective-permute-start | bytes 196616 | tf_op jit(solution)/shard_map/ppermute | solution.py:168
  211.7 7.3 %collective-permute-start.31 = (bf16[16,2048]{1,0:T(8,128)(2,1)S(1)}, bf16[16,2048]{1,0:T(8,128)(2,1)S(1)}, u32[]{:S(2)}, u32[]{:S(2)}) collective-permute-start(bf16[16,2048]{1,0:T(8,128)(2,1)S(1)} %get-tuple-element.80), channel_id=1, source_target_pairs={{0,16},{8,24},{16,0},{24,8},{1,17},{9,25},{17,1},{25,9},{2,18},{10... | collective-permute-start | bytes 196616 | tf_op jit(solution)/shard_map/ppermute | solution.py:168
  212.0 7.0 %collective-permute-start.30 = (bf16[16,2048]{1,0:T(8,128)(2,1)S(1)}, bf16[16,2048]{1,0:T(8,128)(2,1)S(1)}, u32[]{:S(2)}, u32[]{:S(2)}) collective-permute-start(bf16[16,2048]{1,0:T(8,128)(2,1)S(1)} %get-tuple-element.81), channel_id=1, source_target_pairs={{0,8},{8,16},{16,24},{24,0},{1,9},{9,17},{17,25},{25,1},{2,10},{10... | collective-permute-start | bytes 196616 | tf_op jit(solution)/shard_map/ppermute | solution.py:168
  213.0 10.9 %collective-permute-start.23 = (bf16[4,16,2048]{2,1,0:T(8,128)(2,1)S(1)}, bf16[4,16,2048]{2,1,0:T(8,128)(2,1)S(1)}, u32[]{:S(2)}, u32[]{:S(2)}) collective-permute-start(bf16[4,16,2048]{2,1,0:T(8,128)(2,1)S(1)} %get-tuple-element.72), channel_id=1, source_target_pairs={{0,3},{1,0},{2,1},{3,2},{4,7},{5,4},{6,5},{7,6},{8,11},{9,8},{10,9... | collective-permute-start | bytes 786440 | tf_op jit(solution)/shard_map/ppermute | solution.py:168
  214.8 9.3 %collective-permute-start.22 = (bf16[4,16,2048]{2,1,0:T(8,128)(2,1)S(1)}, bf16[4,16,2048]{2,1,0:T(8,128)(2,1)S(1)}, u32[]{:S(2)}, u32[]{:S(2)}) collective-permute-start(bf16[4,16,2048]{2,1,0:T(8,128)(2,1)S(1)} %get-tuple-element.72), channel_id=1, source_target_pairs={{0,2},{1,3},{2,0},{3,1},{4,6},{5,7},{6,4},{7,5},{8,10},{9,11},{10,... | collective-permute-start | bytes 786440 | tf_op jit(solution)/shard_map/ppermute | solution.py:168
  216.9 8.7 %collective-permute-start.21 = (bf16[4,16,2048]{2,1,0:T(8,128)(2,1)S(1)}, bf16[4,16,2048]{2,1,0:T(8,128)(2,1)S(1)}, u32[]{:S(2)}, u32[]{:S(2)}) collective-permute-start(bf16[4,16,2048]{2,1,0:T(8,128)(2,1)S(1)} %get-tuple-element.72), channel_id=1, source_target_pairs={{0,1},{1,2},{2,3},{3,0},{4,5},{5,6},{6,7},{7,4},{8,9},{9,10},{10,1... | collective-permute-start | bytes 786440 | tf_op jit(solution)/shard_map/ppermute | solution.py:168
  219.9 15.8 %collective-permute-start.35 = (bf16[4,16,2048]{2,1,0:T(8,128)(2,1)}, bf16[4,16,2048]{2,1,0:T(8,128)(2,1)}, u32[]{:S(2)}, u32[]{:S(2)}) collective-permute-start(bf16[4,16,2048]{2,1,0:T(8,128)(2,1)} %get-tuple-element.78), channel_id=1, source_target_pairs={{0,3},{1,0},{2,1},{3,2},{4,7},{5,4},{6,5},{7,6},{8,11},{9,8},{10,9... | collective-permute-start | bytes 786440 | tf_op jit(solution)/shard_map/ppermute | solution.py:168
  222.3 14.4 %collective-permute-start.34 = (bf16[4,16,2048]{2,1,0:T(8,128)(2,1)}, bf16[4,16,2048]{2,1,0:T(8,128)(2,1)}, u32[]{:S(2)}, u32[]{:S(2)}) collective-permute-start(bf16[4,16,2048]{2,1,0:T(8,128)(2,1)} %get-tuple-element.78), channel_id=1, source_target_pairs={{0,2},{1,3},{2,0},{3,1},{4,6},{5,7},{6,4},{7,5},{8,10},{9,11},{10,... | collective-permute-start | bytes 786440 | tf_op jit(solution)/shard_map/ppermute | solution.py:168
  223.9 13.0 %collective-permute-start.33 = (bf16[4,16,2048]{2,1,0:T(8,128)(2,1)}, bf16[4,16,2048]{2,1,0:T(8,128)(2,1)}, u32[]{:S(2)}, u32[]{:S(2)}) collective-permute-start(bf16[4,16,2048]{2,1,0:T(8,128)(2,1)} %get-tuple-element.78), channel_id=1, source_target_pairs={{0,1},{1,2},{2,3},{3,0},{4,5},{5,6},{6,7},{7,4},{8,9},{9,10},{10,1... | collective-permute-start | bytes 786440 | tf_op jit(solution)/shard_map/ppermute | solution.py:168
  233.5 14.4 %collective-permute-start.26 = (bf16[64,1296]{1,0:T(8,128)(2,1)}, bf16[64,1296]{1,0:T(8,128)(2,1)S(1)}, u32[]{:S(2)}, u32[]{:S(2)}) collective-permute-start(bf16[64,1296]{1,0:T(8,128)(2,1)} %get-tuple-element.50), channel_id=1, source_target_pairs={{0,24},{8,0},{16,8},{24,16},{1,25},{9,1},{17,9},{25,17},{2,26},{10... | collective-permute-start | bytes 497672 | tf_op jit(solution)/shard_map/ppermute | solution.py:168
  235.6 12.3 %collective-permute-start.25 = (bf16[64,1296]{1,0:T(8,128)(2,1)}, bf16[64,1296]{1,0:T(8,128)(2,1)}, u32[]{:S(2)}, u32[]{:S(2)}) collective-permute-start(bf16[64,1296]{1,0:T(8,128)(2,1)} %get-tuple-element.51), channel_id=1, source_target_pairs={{0,16},{8,24},{16,0},{24,8},{1,17},{9,25},{17,1},{25,9},{2,18},{10... | collective-permute-start | bytes 497672 | tf_op jit(solution)/shard_map/ppermute | solution.py:168
  235.6 12.3 %collective-permute-start.24 = (bf16[64,1296]{1,0:T(8,128)(2,1)}, bf16[64,1296]{1,0:T(8,128)(2,1)}, u32[]{:S(2)}, u32[]{:S(2)}) collective-permute-start(bf16[64,1296]{1,0:T(8,128)(2,1)} %get-tuple-element.49), channel_id=1, source_target_pairs={{0,8},{8,16},{16,24},{24,0},{1,9},{9,17},{17,25},{25,1},{2,10},{10... | collective-permute-start | bytes 497672 | tf_op jit(solution)/shard_map/ppermute | solution.py:168
  244.0 28.1 %copy-start.20 = (f32[8]{0:T(128)S(1)}, f32[8]{0:T(128)}, u32[]{:S(2)}) copy-start(f32[8]{0:T(128)} %get-tuple-element.86) | copy-start | bytes 100
  244.0 28.1 %copy-start.28 = (f32[8]{0:T(128)S(1)}, f32[8]{0:T(128)}, u32[]{:S(2)}) copy-start(f32[8]{0:T(128)} %get-tuple-element.87) | copy-start | bytes 100
  244.0 30.9 %copy-start.18 = (f32[128]{0:T(128)S(1)}, f32[128]{0:T(128)}, u32[]{:S(2)}) copy-start(f32[128]{0:T(128)} %get-tuple-element.117) | copy-start | bytes 1540
  245.2 32.4 %copy-start.19 = (f32[128]{0:T(128)S(1)}, f32[128]{0:T(128)}, u32[]{:S(2)}) copy-start(f32[128]{0:T(128)} %get-tuple-element.118) | copy-start | bytes 1540
  245.3 32.5 %copy-start.14 = (pred[128,128]{1,0:T(8,128)(4,1)S(1)}, pred[128,128]{1,0:T(8,128)(4,1)}, u32[]{:S(2)}) copy-start(pred[128,128]{1,0:T(8,128)(4,1)} %fusion.140) | copy-start | bytes 49156
  245.3 15.3 %collective-permute-start.38 = (bf16[64,1296]{1,0:T(8,128)(2,1)S(1)}, bf16[64,1296]{1,0:T(8,128)(2,1)S(1)}, u32[]{:S(2)}, u32[]{:S(2)}) collective-permute-start(bf16[64,1296]{1,0:T(8,128)(2,1)S(1)} %get-tuple-element.53), channel_id=1, source_target_pairs={{0,24},{8,0},{16,8},{24,16},{1,25},{9,1},{17,9},{25,17},{2,26},{10... | collective-permute-start | bytes 497672 | tf_op jit(solution)/shard_map/ppermute | solution.py:168
  247.5 19.8 %collective-permute-start.37 = (bf16[64,1296]{1,0:T(8,128)(2,1)S(1)}, bf16[64,1296]{1,0:T(8,128)(2,1)S(1)}, u32[]{:S(2)}, u32[]{:S(2)}) collective-permute-start(bf16[64,1296]{1,0:T(8,128)(2,1)S(1)} %get-tuple-element.54), channel_id=1, source_target_pairs={{0,16},{8,24},{16,0},{24,8},{1,17},{9,25},{17,1},{25,9},{2,18},{10... | collective-permute-start | bytes 497672 | tf_op jit(solution)/shard_map/ppermute | solution.py:168
  247.9 19.4 %collective-permute-start.36 = (bf16[64,1296]{1,0:T(8,128)(2,1)S(1)}, bf16[64,1296]{1,0:T(8,128)(2,1)}, u32[]{:S(2)}, u32[]{:S(2)}) collective-permute-start(bf16[64,1296]{1,0:T(8,128)(2,1)S(1)} %get-tuple-element.52), channel_id=1, source_target_pairs={{0,8},{8,16},{16,24},{24,0},{1,9},{9,17},{17,25},{25,1},{2,10},{10... | collective-permute-start | bytes 497672 | tf_op jit(solution)/shard_map/ppermute | solution.py:168
  249.0 29.1 %copy-start.21 = (f32[8]{0:T(128)S(1)}, f32[8]{0:T(128)}, u32[]{:S(2)}) copy-start(f32[8]{0:T(128)} %get-tuple-element.85) | copy-start | bytes 100
  268.5 10.7 %copy-start.27 = (f32[128]{0:T(128)S(1)}, f32[128]{0:T(128)}, u32[]{:S(2)}) copy-start(f32[128]{0:T(128)} %compare_convert_fusion.1) | copy-start | bytes 1540
  285.7 15.3 %collective-permute-start.41 = (bf16[16,8192]{1,0:T(8,128)(2,1)S(1)}, bf16[16,8192]{1,0:T(8,128)(2,1)S(1)}, u32[]{:S(2)}, u32[]{:S(2)}) collective-permute-start(bf16[16,8192]{1,0:T(8,128)(2,1)S(1)} %get-tuple-element.33), channel_id=1, source_target_pairs={{0,3},{1,0},{2,1},{3,2},{4,7},{5,4},{6,5},{7,6},{8,11},{9,8},{10,9... | collective-permute-start | bytes 786440 | tf_op jit(solution)/shard_map/ppermute | solution.py:168
  291.3 12.6 %collective-permute-start.40 = (bf16[16,8192]{1,0:T(8,128)(2,1)S(1)}, bf16[16,8192]{1,0:T(8,128)(2,1)S(1)}, u32[]{:S(2)}, u32[]{:S(2)}) collective-permute-start(bf16[16,8192]{1,0:T(8,128)(2,1)S(1)} %get-tuple-element.34), channel_id=1, source_target_pairs={{0,2},{1,3},{2,0},{3,1},{4,6},{5,7},{6,4},{7,5},{8,10},{9,11},{10,... | collective-permute-start | bytes 786440 | tf_op jit(solution)/shard_map/ppermute | solution.py:168
  291.3 12.6 %collective-permute-start.39 = (bf16[16,8192]{1,0:T(8,128)(2,1)S(1)}, bf16[16,8192]{1,0:T(8,128)(2,1)S(1)}, u32[]{:S(2)}, u32[]{:S(2)}) collective-permute-start(bf16[16,8192]{1,0:T(8,128)(2,1)S(1)} %get-tuple-element.32), channel_id=1, source_target_pairs={{0,1},{1,2},{2,3},{3,0},{4,5},{5,6},{6,7},{7,4},{8,9},{9,10},{10,1... | collective-permute-start | bytes 786440 | tf_op jit(solution)/shard_map/ppermute | solution.py:168
  296.7 20.3 %copy-start.7 = (bf16[4,2,16,2048]{3,2,1,0:T(8,128)(2,1)S(1)}, bf16[4,2,16,2048]{3,2,1,0:T(8,128)(2,1)}, u32[]{:S(2)}) copy-start(bf16[4,2,16,2048]{3,2,1,0:T(8,128)(2,1)} %maximum_bitcast_fusion) | copy-start | bytes 1572868
  297.6 10.5 %collective-permute-start.29 = (bf16[16,8192]{1,0:T(8,128)(2,1)}, bf16[16,8192]{1,0:T(8,128)(2,1)S(1)}, u32[]{:S(2)}, u32[]{:S(2)}) collective-permute-start(bf16[16,8192]{1,0:T(8,128)(2,1)} %get-tuple-element.30), channel_id=1, source_target_pairs={{0,3},{1,0},{2,1},{3,2},{4,7},{5,4},{6,5},{7,6},{8,11},{9,8},{10,9... | collective-permute-start | bytes 786440 | tf_op jit(solution)/shard_map/ppermute | solution.py:168
  299.6 15.9 %collective-permute-start.28 = (bf16[16,8192]{1,0:T(8,128)(2,1)}, bf16[16,8192]{1,0:T(8,128)(2,1)S(1)}, u32[]{:S(2)}, u32[]{:S(2)}) collective-permute-start(bf16[16,8192]{1,0:T(8,128)(2,1)} %get-tuple-element.31), channel_id=1, source_target_pairs={{0,2},{1,3},{2,0},{3,1},{4,6},{5,7},{6,4},{7,5},{8,10},{9,11},{10,... | collective-permute-start | bytes 786440 | tf_op jit(solution)/shard_map/ppermute | solution.py:168
  301.0 14.4 %collective-permute-start.27 = (bf16[16,8192]{1,0:T(8,128)(2,1)S(1)}, bf16[16,8192]{1,0:T(8,128)(2,1)}, u32[]{:S(2)}, u32[]{:S(2)}) collective-permute-start(bf16[16,8192]{1,0:T(8,128)(2,1)S(1)} %get-tuple-element.29), channel_id=1, source_target_pairs={{0,1},{1,2},{2,3},{3,0},{4,5},{5,6},{6,7},{7,4},{8,9},{9,10},{10,1... | collective-permute-start | bytes 786440 | tf_op jit(solution)/shard_map/ppermute | solution.py:168
  (10 other events, 24.0 us)
Sparse Core Ops, SparseCore 0:
  8.9 25.0 all-gather.6
  35.6 31.2 all-gather.8
where the time goes:
time: 346 us; the launch traced here: 344 us
  Pallas kernels  69.9 us (20%)
  matrix products  48.2 us (14%)
  starting transfers between devices  47 us (14%)
  waiting for transfers between devices  46.6 us (13%)
  blocking collectives  39.7 us (11%)
  other arithmetic  39 us (11%)
  local copies, waits for them, and re-layouts  38.3 us (11%)
  between operations  15.4 us (4%)
    pallas_call x4, Pallas kernels, remote_call(): pl.pallas_call(kernel, out_shape=out_shape, in_specs=[anywhere] * len(ope...  54.3 us
    ppermute x42, starting transfers between devices, shift(): lax.ppermute(block, axis, [(i, (i + distance) % n) for i in range(n)])  47 us
    ppermute x42, waiting for transfers between devices, shift(): lax.ppermute(block, axis, [(i, (i + distance) % n) for i in range(n)])  45.2 us
    all_gather x4, blocking collectives, mix(): proj = lax.all_gather(proj, 'section', axis=0, tiled=True)  21.5 us
    dot_general x4, matrix products, mix(): jnp.dot(normed, w_out[layer], preferred_element_type=f32).astype(bf16)  19.9 us
    dot_general x4, matrix products, project(): proj = jnp.dot(flat, w_in[layer], preferred_element_type=f32).astype(bf16)  18.6 us
    all_gather x4, blocking collectives, mix(): pre = lax.all_gather(pre, 'section', axis=0, tiled=True)  18.3 us
    pallas_call x1, Pallas kernels, deliver(): pl.pallas_call(kernel, out_shape=out_shape, in_specs=[anywhere] * cores,...  15.6 us
  transfers between devices with their start and end apart: 44, of which 16 were waited for; matrix products, arithmetic and copies ran while one was open for 30% of the time, Pallas kernels for 16%

commit v1 on v0

v1 whole, which is shorter than its diff:
```python
import jax
import jax.numpy as jnp
from jax import lax
from jax.experimental import pallas as pl
from jax.experimental.pallas import tpu as pltpu
from jax.sharding import PartitionSpec as P

HEAD_DIM = 64
STATE = 128
HEADS_DEV = 8
SPAN = 64
LANES = 128
TILE = 256
FEW = 16

epsilon = 1e-05
MESH = pl.DeviceIdType.MESH
F32, BF16 = jnp.float32, jnp.bfloat16


def rows(start, size):
    return pl.ds(pl.multiple_of(start, FEW), size)


def cols(start, size):
    return pl.ds(pl.multiple_of(start, LANES), size)


def nt_dot(a, b, precision=None):
    return lax.dot_general(
        a, b, (((1,), (1,)), ((), ())), precision=precision, preferred_element_type=F32
    )


def tn_dot(a, b):
    return lax.dot_general(a, b, (((0,), (0,)), ((), ())), preferred_element_type=F32)


def exact_dot(a, b):
    return jnp.dot(a, b, precision=lax.Precision.HIGHEST, preferred_element_type=F32)


def relay(
    tokens, dest_slot, resets, gain, w_in, w_step, step_bias, a_log, d_skip, out_gain, w_out
):
    groups, width, cores = lax.axis_size("dp"), lax.axis_size("tensor"), lax.axis_size("section")
    row_count, feat_local = tokens.shape
    feats = feat_local * width
    depth, n_cols = w_in.shape
    head_cols = HEADS_DEV * HEAD_DIM
    chunks = max(1, row_count // (FEW * width))
    chunk = row_count // chunks
    few = chunk // width
    quarter = row_count // width
    spans = chunk // SPAN
    total = groups * row_count
    flat = groups * chunk
    m_block = min(flat, TILE)

    def kernel(
        tok, slot_in, rst, gain, w_in_hbm, w_step, step_bias, a_log, d_skip, out_gain, w_out_hbm,
        out,
        w_in, w_out, T, X, sc, sl, oh, scol, U, XR, Y, YR, S, SR, PO, PR, hin, ho, un,
        state, consts, gated_s, normed_s,
        w_sem, l_sem, o_sem,
        a1_s, a1_r, sl_s, sl_r, a2_s, a2_r, c2_s, c2_r, a3_s, a3_r, c3_s, c3_r,
        y_s, y_r, p_s, p_r, k_s, k_r, o_s, o_r, h_s, h_r, d_s, d_r, z_s, z_r, g_s, g_r,
    ):
        group, lane, core = lax.axis_index("dp"), lax.axis_index("tensor"), lax.axis_index("section")
        first, last = core == 0, core == cores - 1

        def up(k):
            return lax.rem(group + k, groups)

        def down(k):
            return lax.rem(group + groups - k, groups)

        def right(k):
            return lax.rem(lane + k, width)

        def left(k):
            return lax.rem(lane + width - k, width)

        def send(src, dst, ss, rs, device):
            return pltpu.make_async_remote_copy(
                src_ref=src, dst_ref=dst, send_sem=ss, recv_sem=rs,
                device_id=device, device_id_type=MESH,
            )

        in_plane = range(1, width)
        in_line = range(1, groups)

        barrier = pltpu.get_barrier_semaphore()
        for k in in_plane:
            pl.semaphore_signal(barrier, inc=1, device_id={"tensor": right(k)}, device_id_type=MESH)
        for k in in_line:
            pl.semaphore_signal(barrier, inc=1, device_id={"dp": up(k)}, device_id_type=MESH)
        for k in range(1, cores):
            pl.semaphore_signal(
                barrier, inc=1, device_id={"section": lax.rem(core + k, cores)}, device_id_type=MESH
            )
        pl.semaphore_wait(barrier, width + groups + cores - 3)

        def a1(k):
            return send(
                tok.at[rows(right(k) * quarter, quarter), :],
                T.at[:, cols(lane * feat_local, feat_local)],
                a1_s.at[k - 1], a1_r.at[k - 1], {"tensor": right(k)},
            )

        def a1_in(k):
            return send(
                tok.at[rows(lane * quarter, quarter), :],
                T.at[:, cols(left(k) * feat_local, feat_local)],
                a1_s.at[k - 1], a1_r.at[k - 1], {"tensor": right(k)},
            )

        def slots(k, at):
            return send(slot_in, sl.at[at], sl_s.at[k - 1], sl_r.at[k - 1], {"dp": up(k)})

        def x_piece(s, q):
            return X.at[rows(s * row_count + q * quarter, quarter), :]

        def a2(k, at):
            return send(
                T.at[:, cols(up(k) * depth, depth)], x_piece(at, lane),
                a2_s.at[k - 1], a2_r.at[k - 1], {"dp": up(k)},
            )

        def c2(k, at):
            return send(
                sc.at[lane, group], sc.at[lane, at], c2_s.at[k - 1], c2_r.at[k - 1], {"dp": up(k)}
            )

        def a3(j, k, at):
            return send(
                x_piece(down(j), lane), x_piece(down(j), at),
                a3_s.at[j, k - 1], a3_r.at[j, k - 1], {"tensor": right(k)},
            )

        def c3(k, at):
            return send(sc.at[lane], sc.at[at], c3_s.at[k - 1], c3_r.at[k - 1], {"tensor": right(k)})

        def proj_out(c, k):
            return send(
                Y.at[c, rows(up(k) * chunk, chunk), :], YR.at[c, k - 1],
                y_s.at[c, k - 1], y_r.at[c, k - 1], {"dp": up(k)},
            )

        def side_out(c, k):
            return send(
                S.at[c, up(k)], SR.at[c, k - 1],
                p_s.at[c, k - 1], p_r.at[c, k - 1], {"dp": up(k)},
            )

        def kept_out(c, k, at):
            return send(
                XR.at[c, rows(up(k) * chunk + lane * few, few), :],
                hin.at[c, :, cols(at * depth, depth)],
                k_s.at[c, k - 1], k_r.at[c, k - 1], {"dp": up(k)},
            )

        def part_out(c, k):
            return send(
                PO.at[c, rows(right(k) * few, few), :], PR.at[c, k - 1],
                o_s.at[c, k - 1], o_r.at[c, k - 1], {"tensor": right(k)},
            )

        def hand_over(c):
            return send(
                ho.at[c], hin.at[c], h_s.at[c], h_r.at[c], {"section": lax.rem(core + 1, cores)}
            )

        def out_rows(c, q):
            return out.at[rows(c * chunk + q * few, few), :]

        def deliver(c, k, at):
            return send(
                ho.at[c, :, cols(right(k) * feat_local, feat_local)], out_rows(c, at),
                d_s.at[c, k - 1], d_r.at[c, k - 1], {"tensor": right(k)},
            )

        def keep(c):
            return pltpu.make_async_copy(
                ho.at[c, :, cols(lane * feat_local, feat_local)], out_rows(c, lane), o_sem.at[c]
            )

        def u_piece(c, s, q):
            return U.at[c, rows(s * chunk + q * few, few), :]

        def z_out(c, k, at):
            return send(
                un.at[c, :, cols(up(k) * depth, depth)], u_piece(c, at, lane),
                z_s.at[c, k - 1], z_r.at[c, k - 1], {"dp": up(k)},
            )

        def spread(c, j, k, at):
            return send(
                u_piece(c, down(j), lane), u_piece(c, down(j), at),
                g_s.at[c, j, k - 1], g_r.at[c, j, k - 1], {"tensor": right(k)},
            )

        own_t = pltpu.make_async_copy(
            tok.at[rows(lane * quarter, quarter), :],
            T.at[:, cols(lane * feat_local, feat_local)], l_sem.at[0],
        )
        own_x = pltpu.make_async_copy(
            T.at[:, cols(group * depth, depth)], x_piece(group, lane), l_sem.at[1]
        )
        load_in = pltpu.make_async_copy(w_in_hbm, w_in, w_sem.at[0])
        load_out = pltpu.make_async_copy(w_out_hbm, w_out, w_sem.at[1])

        @pl.when(first)
        def _():
            for k in in_plane:
                a1(k).start()
            own_t.start()
            for k in in_line:
                slots(k, group).start()

        load_in.start()
        load_out.start()

        row_at = lax.broadcasted_iota(jnp.int32, (LANES, LANES), 0)
        lane_at = lax.broadcasted_iota(jnp.int32, (LANES, LANES), 1)
        low = lane_at < SPAN
        inner = jnp.where(low, lane_at, lane_at - SPAN)
        consts[0] = ((row_at < SPAN) & (row_at <= inner)).astype(F32)
        consts[1] = ((row_at < SPAN) & (row_at == inner)).astype(F32)
        consts[2] = (lane_at <= row_at).astype(F32)
        consts[3] = (lane_at == row_at).astype(F32)
        state[...] = jnp.zeros_like(state)
        S[...] = jnp.zeros_like(S)

        @pl.when(first)
        def _():
            sl[group] = slot_in[...]
            own_t.wait()
            for k in in_plane:
                a1_in(k).wait_recv()
            for k in in_line:
                a2(k, group).start()
            own_x.start()
            wide = T[...].astype(F32)
            scale = lax.rsqrt(jnp.mean(wide * wide, axis=-1, keepdims=True) + epsilon)
            own_x.wait()
            for k in in_plane:
                a3(0, k, lane).start()
            spot = lax.rem(lane * quarter, LANES)
            i_at = lax.broadcasted_iota(jnp.int32, (quarter, LANES), 0)
            l_at = lax.broadcasted_iota(jnp.int32, (quarter, LANES), 1)
            line = jnp.sum(jnp.where(l_at == i_at + spot, scale, 0.0), axis=0, keepdims=True)
            sc[lane, group] = jnp.broadcast_to(line, (8, LANES))
            for k in in_line:
                c2(k, group).start()
            for j in in_line:
                a2(j, down(j)).wait_recv()
                for k in in_plane:
                    a3(j, k, lane).start()
            for j in in_line:
                c2(j, down(j)).wait_recv()
            for k in in_plane:
                c3(k, lane).start()
            for j in in_line:
                slots(j, down(j)).wait_recv()
            for k in in_plane:
                c3(k, left(k)).wait_recv()
                for j in range(groups):
                    a3(j, k, left(k)).wait_recv()

        load_in.wait()
        load_out.wait()

        def permute(c):
            for g in range(groups):
                wanted = (
                    g * row_count + c * chunk
                    + lax.broadcasted_iota(jnp.int32, (chunk, LANES), 0)
                )
                found = jnp.zeros((chunk, LANES), F32)
                for tile in range(total // LANES):
                    s, at = tile * LANES // row_count, tile * LANES % row_count
                    mask = sl[s, at // LANES : at // LANES + 1, :] == wanted
                    oh[g * chunk : (g + 1) * chunk, tile * LANES : (tile + 1) * LANES] = jnp.where(
                        mask, 1.0, 0.0
                    ).astype(BF16)
                    line = sc[at // quarter, s, 0:1, :]
                    for q in range(1, LANES // quarter):
                        line = line + sc[at // quarter + q, s, 0:1, :]
                    found = found + jnp.where(mask, line, 0.0)
                scol[g * chunk : (g + 1) * chunk, :] = jnp.broadcast_to(
                    jnp.sum(found, axis=1, keepdims=True), (chunk, LANES)
                )

            @pl.loop(0, flat // m_block)
            def _(m):
                here = rows(m * m_block, m_block)

                @pl.loop(0, depth // TILE)
                def _(n):
                    there = cols(n * TILE, TILE)
                    x = jnp.dot(oh[here, :], X[:, there], preferred_element_type=F32)
                    XR[c, here, there] = x.astype(BF16)
                    u = x * scol[here, 0:1] * gain[:, cols(group * depth + n * TILE, TILE)]
                    U[c, here, there] = u.astype(BF16)

            hin[c, :, cols(group * depth, depth)] = XR[c, rows(group * chunk + lane * few, few), :]
            for k in in_line:
                kept_out(c, k, group).start()

        def project(c):
            @pl.loop(0, flat // m_block)
            def _(m):
                here = rows(m * m_block, m_block)

                @pl.loop(0, n_cols // TILE)
                def _(n):
                    there = cols(n * TILE, TILE)
                    Y[c, here, there] = jnp.dot(
                        U[c, here, :], w_in[:, there], preferred_element_type=F32
                    ).astype(BF16)

            for g in range(groups):
                for b in range(spans):
                    at = g * chunk + b * SPAN
                    S[c, g, b, :, 0:SPAN] = nt_dot(w_step[...], U[c, at : at + SPAN, :])
            for k in in_line:
                side_out(c, k).start()
                proj_out(c, k).start()

        def scan_span(c, b):
            at = b * SPAN
            proj = Y[c, rows(group * chunk + at, SPAN), :].astype(F32)
            pre = S[c, group, b]
            for k in in_line:
                proj = proj + YR[c, k - 1, at : at + SPAN, :].astype(F32)
                pre = pre + SR[c, k - 1, b]
            proj = proj.astype(BF16)
            step = pre + step_bias[...]
            step = jnp.maximum(step, 0.0) + jnp.log1p(jnp.exp(-jnp.abs(step)))
            decay = -jnp.exp(a_log[...]) * step
            reset = rst[c * spans + b]
            to_rows, dup = consts[0], consts[1]
            to_cols, eye = consts[2][:SPAN], consts[3][:SPAN]
            hp = lax.Precision.HIGHEST
            cum_row, step_row, seg_row = (
                exact_dot(decay, to_rows), exact_dot(step, dup), exact_dot(reset, to_rows)
            )
            cum, step_col, seg = (
                nt_dot(to_cols, decay, hp), nt_dot(eye, step, hp), nt_dot(to_cols, reset, hp)
            )
            l_at = lax.broadcasted_iota(jnp.int32, (SPAN, LANES), 1)
            t_at = lax.broadcasted_iota(jnp.int32, (SPAN, LANES), 0)
            low = l_at < SPAN
            inside = (seg[:, 0:1] == seg_row[0:1, :]) & (t_at >= jnp.where(low, l_at, l_at - SPAN))
            top = cum[SPAN - 1 : SPAN, :]
            last_seg = seg[SPAN - 1 : SPAN, :]
            carry = jnp.where(seg == 0.0, jnp.exp(cum), 0.0)
            tail = jnp.where(seg == last_seg, jnp.exp(top - cum), 0.0) * step_col
            hold = jnp.where(last_seg == 0.0, jnp.exp(top), 0.0)
            writes = proj[:, 2 * head_cols : 2 * head_cols + STATE]
            reads = proj[:, 2 * head_cols + STATE :]
            scores = nt_dot(reads, jnp.concatenate([writes, writes], axis=0))
            squares = jnp.zeros((SPAN, LANES), F32)
            for j in range(head_cols // LANES):
                a, z = 2 * j, 2 * j + 1
                part = slice(j * LANES, (j + 1) * LANES)

                def pair_col(v):
                    return jnp.where(low, v[:, a : a + 1], v[:, z : z + 1])

                def pair_row(v):
                    return jnp.where(low[0:1], v[a : a + 1, :], v[z : z + 1, :])

                x = proj[:, head_cols + j * LANES : head_cols + (j + 1) * LANES].astype(F32)
                gap = jnp.where(inside, pair_col(cum) - pair_row(cum_row), 0.0)
                weights = jnp.where(inside, jnp.exp(gap), 0.0) * scores * pair_row(step_row)
                both = jnp.concatenate(
                    [jnp.where(low, x, 0.0), jnp.where(low, 0.0, x)], axis=0
                ).astype(BF16)
                y = jnp.dot(weights.astype(BF16), both, preferred_element_type=F32)
                held = state[:, part]
                y = y + pair_col(carry) * jnp.dot(
                    reads, held.astype(BF16), preferred_element_type=F32
                )
                y = y + d_skip[:, part] * x
                fresh = tn_dot(writes, (pair_col(tail) * x).astype(BF16))
                keep_by = jnp.where(low[0:1], hold[:, a : a + 1], hold[:, z : z + 1])
                state[:, part] = fresh + keep_by * held
                gate = proj[:, part].astype(F32)
                gated = y * (gate * lax.logistic(gate))
                squares = squares + gated * gated
                gated_s[:, part] = gated
            mean = jnp.sum(squares, axis=1, keepdims=True) / head_cols
            normed = gated_s[...] * lax.rsqrt(mean + epsilon) * out_gain[...]
            normed_s[at : at + SPAN, :] = normed.astype(BF16)

        def mix(c):
            for k in in_line:
                side_out(c, k).wait_recv()
                proj_out(c, k).wait_recv()
            for b in range(spans):
                scan_span(c, b)

            @pl.loop(0, feats // TILE)
            def _(n):
                there = cols(n * TILE, TILE)
                PO[c, :, there] = jnp.dot(
                    normed_s[...], w_out[:, there], preferred_element_type=F32
                ).astype(BF16)

            for k in in_plane:
                part_out(c, k).start()

        def finish(c):
            for k in in_plane:
                part_out(c, k).wait_recv()

            @pl.when(first)
            def _():
                for k in in_line:
                    kept_out(c, k, down(k)).wait_recv()

            @pl.loop(0, feats // (4 * TILE))
            def _(n):
                there = cols(n * 4 * TILE, 4 * TILE)
                added = PO[c, rows(lane * few, few), there].astype(F32)
                for k in in_plane:
                    added = added + PR[c, k - 1, :, there].astype(F32)
                ho[c, :, there] = (hin[c, :, there].astype(F32) + added).astype(BF16)

            @pl.when(jnp.logical_not(last))
            def _():
                hand_over(c).start()

            for k in in_plane:
                deliver(c, k, lane).start()
            keep(c).start()

        def normalise(c):
            hand_over(c).wait_recv()
            wide = hin[c].astype(F32)
            scale = lax.rsqrt(jnp.mean(wide * wide, axis=-1, keepdims=True) + epsilon)
            un[c] = (wide * scale * gain[...]).astype(BF16)
            for k in in_line:
                z_out(c, k, group).start()
            U[c, rows(group * chunk + lane * few, few), :] = un[c, :, cols(group * depth, depth)]
            for k in in_plane:
                spread(c, 0, k, lane).start()

        def forward(c):
            for j in in_line:
                z_out(c, j, down(j)).wait_recv()
                for k in in_plane:
                    spread(c, j, k, lane).start()

        def gathered(c):
            for k in in_plane:
                for j in range(groups):
                    spread(c, j, k, left(k)).wait_recv()

        mix_lag = jnp.where(first, 2, 1)
        end_lag = jnp.where(first, 3, 1)

        def turn(i, _):
            fresh = i < chunks

            @pl.when(fresh & jnp.logical_not(first))
            def _():
                normalise(i)

            m = i - mix_lag

            @pl.when((m >= 0) & (m < chunks))
            def _():
                mix(m)

            @pl.when(fresh & jnp.logical_not(first))
            def _():
                forward(i)

            e = i - end_lag

            @pl.when((e >= 0) & (e < chunks))
            def _():
                finish(e)

            @pl.when(fresh & first)
            def _():
                permute(i)

            @pl.when(fresh & jnp.logical_not(first))
            def _():
                gathered(i)

            @pl.when(fresh)
            def _():
                project(i)

            return 0

        lax.fori_loop(0, chunks + 3, turn, 0)

        def settle(c, _):
            keep(c).wait()
            for k in in_plane:
                deliver(c, k, left(k)).wait_recv()
                deliver(c, k, lane).wait_send()
                part_out(c, k).wait_send()
            for k in in_line:
                side_out(c, k).wait_send()
                proj_out(c, k).wait_send()

            @pl.when(first)
            def _():
                for k in in_line:
                    kept_out(c, k, group).wait_send()

            @pl.when(jnp.logical_not(first))
            def _():
                for k in in_line:
                    z_out(c, k, group).wait_send()
                for k in in_plane:
                    for j in range(groups):
                        spread(c, j, k, lane).wait_send()

            @pl.when(jnp.logical_not(last))
            def _():
                hand_over(c).wait_send()

            return 0

        lax.fori_loop(0, chunks, settle, 0)

        @pl.when(first)
        def _():
            for k in in_line:
                slots(k, group).wait_send()
                a2(k, group).wait_send()
                c2(k, group).wait_send()
            for k in in_plane:
                a1(k).wait_send()
                c3(k, lane).wait_send()
                for j in range(groups):
                    a3(j, k, lane).wait_send()

    vmem, dma = pltpu.VMEM, pltpu.SemaphoreType.DMA
    near, line = (width - 1,), (groups - 1,)
    scratch = [
        vmem((depth, n_cols), BF16),
        vmem((head_cols, feats), BF16),
        vmem((quarter, feats), BF16),
        vmem((total, depth), BF16),
        vmem((width, groups, 8, LANES), F32),
        vmem((groups, row_count // LANES, LANES), jnp.int32),
        vmem((flat, total), BF16),
        vmem((flat, LANES), F32),
        vmem((chunks, flat, depth), BF16),
        vmem((chunks, flat, depth), BF16),
        vmem((chunks, flat, n_cols), BF16),
        vmem((chunks, groups - 1, chunk, n_cols), BF16),
        vmem((chunks, groups, spans, 8, LANES), F32),
        vmem((chunks, groups - 1, spans, 8, LANES), F32),
        vmem((chunks, chunk, feats), BF16),
        vmem((chunks, width - 1, few, feats), BF16),
        vmem((chunks, few, feats), BF16),
        vmem((chunks, few, feats), BF16),
        vmem((chunks, few, feats), BF16),
        vmem((STATE, head_cols), F32),
        vmem((4, LANES, LANES), F32),
        vmem((SPAN, head_cols), F32),
        vmem((chunk, head_cols), BF16),
        dma((2,)), dma((2,)), dma((chunks,)),
    ]
    for shape in [
        near, line, line, line, (groups,) + near, near,
        (chunks,) + line, (chunks,) + line, (chunks,) + line, (chunks,) + near,
        (chunks,), (chunks,) + near, (chunks,) + line, (chunks, groups) + near,
    ]:
        scratch += [dma(shape), dma(shape)]
    anywhere = pl.BlockSpec(memory_space=pl.ANY)
    held = pl.BlockSpec(memory_space=pltpu.VMEM)
    return pl.pallas_call(
        kernel,
        out_shape=jax.ShapeDtypeStruct((row_count, feat_local), BF16),
        in_specs=[
            anywhere, held, held, held, anywhere, held, held, held, held, held, anywhere
        ],
        out_specs=anywhere,
        scratch_shapes=scratch,
        compiler_params=pltpu.CompilerParams(
            collective_id=0, has_side_effects=True, vmem_limit_bytes=63 * 1024 * 1024
        ),
    )(tokens, dest_slot, resets, gain, w_in, w_step, step_bias, a_log, d_skip, out_gain, w_out)


def per_device(
    tokens, dest_slot, doc_reset, norm_gain, w_in, w_step, step_bias, a_log, d_skip, out_gain, w_out
):
    group = lax.axis_index("dp")
    row_count = tokens.shape[0]
    depth = w_in.shape[1]
    own_step = lax.dynamic_slice_in_dim(w_step[0], group * depth, depth, axis=0).T
    resets = doc_reset.astype(F32).reshape(-1, 1, SPAN)
    resets = jnp.broadcast_to(jnp.pad(resets, ((0, 0), (0, 0), (0, LANES - SPAN))),
                              (row_count // SPAN, 8, LANES))
    out = relay(
        tokens,
        dest_slot.reshape(-1, LANES),
        resets,
        norm_gain,
        w_in[0],
        own_step,
        step_bias.reshape(-1, 1),
        a_log.reshape(-1, 1),
        jnp.repeat(d_skip, HEAD_DIM, axis=1),
        out_gain,
        w_out[0],
    )
    return out[None]


def solution(mesh):
    placed = (
        P("dp", "tensor"),
        P("dp"),
        P("dp"),
        P("section", None),
        P("section", "dp", "tensor"),
        P("section", None, "tensor"),
        P("section", "tensor"),
        P("section", "tensor"),
        P("section", "tensor"),
        P("section", "tensor"),
        P("section", "tensor", None),
    )
    return jax.shard_map(
        per_device,
        mesh=mesh,
        in_specs=placed,
        out_specs=P("section", "dp", "tensor"),
        check_vma=False,
    )
```

time: 346 us -> 224 us (0.65)
  Pallas kernels: 69.9 us -> 215 us
  matrix products: 48.2 us -> 0 us
  starting transfers between devices: 47 us -> 0 us
  waiting for transfers between devices: 46.6 us -> 0 us
  blocking collectives: 39.7 us -> 0 us
  other arithmetic: 39 us -> 0.72 us
  local copies, waits for them, and re-layouts: 38.3 us -> 7.64 us
  between operations: 15.4 us -> 0.01 us
    pallas_call x5 -> x1, Pallas kernels: 69.9 us -> 215 us  [relay(): pl.pallas_call(kernel, out_shape=jax.ShapeDtypeStruct((row_count, feat_lo...]
    dot_general x24 -> x0, matrix products: 48.2 us -> none  [the longest x4 19.9 us: mix(): jnp.dot(normed, w_out[layer], preferred_element_type=f32).astype(bf16)]
    ppermute x42 -> x0, starting transfers between devices: 47 us -> none  [shift(): lax.ppermute(block, axis, [(i, (i + distance) % n) for i in range(n)])]
    ppermute x42 -> x0, waiting for transfers between devices: 45.2 us -> none  [shift(): lax.ppermute(block, axis, [(i, (i + distance) % n) for i in range(n)])]
    all_gather x8 -> x0, blocking collectives: 39.7 us -> none  [the longest x4 21.5 us: mix(): proj = lax.all_gather(proj, 'section', axis=0, tiled=True)]
    another operation x20 -> x0, other arithmetic: 15.8 us -> none  [the longest x2 7.13 us: per_device(): pool = jnp.stack(pool).reshape(-1, depth)]
    slice x27 -> x0, local copies, waits for them, and re-layouts: 11 us -> none  [the longest x2 3.26 us: per_device(): kept = exchange([kept[k] for k in range(groups)], 'dp')]
    gather x1 -> x0, local copies, waits for them, and re-layouts: 7.13 us -> none  [per_device(): first = pool[place].reshape(CHUNKS, groups, part, depth)]
  transfers between devices with their start and end apart: 44 -> 0, of which waited for: 16 -> 0; matrix products, arithmetic and copies ran while one was open for 30% -> 0% of each run, Pallas kernels for 16% -> 0%
where the time goes in v1:
time: 224 us; the launch traced here: 223 us
  Pallas kernels  215 us (96%)
  local copies, waits for them, and re-layouts  7.64 us (3%)
    pallas_call x1, Pallas kernels, relay(): pl.pallas_call(kernel, out_shape=jax.ShapeDtypeStruct((row_count, feat_lo...  215 us

profile of v1, /device:TPU:1, one launch (start us, length us, event | category | flops | bytes accessed | tf_op | source)
XLA Modules:
  0.0 223.5 jit_solution(12309598310831250053)
XLA Ops:
  0.0 0.0 copy-start
  0.0 0.7 convert_element_type.5
  0.7 0.1 reshape.19
  0.8 1.3 copy.12.step_bias
  2.1 1.3 copy.13.a_log
  3.4 0.7 broadcast_in_dim.17
  4.2 0.7 broadcast_in_dim.18.d_skip
  4.8 0.6 broadcast_in_dim.16.rst
  5.4 0.0 copy-done
  5.4 0.6 dynamic-slice_bitcast_fusion.w_step
  6.1 215.1 %shard_map.112 = bf16[256,2048]{1,0:T(8,128)(2,1)} custom-call(bf16[256,2048]{1,0:T(8,128)(2,1)} %tok.1, s32[2,128]{1,0:T(2,128)} %bitcast.16, f32[4,8,128]{2,1,0:T(8,128)} %broadcast_in_dim.16.rst, f32[1,8192]{1,0:T(1,128)} %gain.1, bf16[2048,1280]{1,0:T(8,128)(2,1)} %bitcast.14, bf16[8,2048]{1,0:T(8,128)(2,1)} %dynamic-slice_bitcast_fusion.w_step, ...), custom_call_target="tpu_custom_call" | custom-call | tf_op jit(solution)/shard_map/pallas_call | solution.py:583
  221.2 2.3 %copy.15 = bf16[1,256,2048]{2,1,0:T(8,128)(2,1)} copy(bf16[1,256,2048]{2,1,0:T(8,128)(2,1)} %bitcast.15) | data formatting | bytes 2097152
  (1 shorter events, 0.0 us)
Async XLA Ops:
  0.0 5.4 %copy-start = (bf16[1,8192,8]{1,2,0:T(8,128)(2,1)S(1)}, bf16[1,8192,8]{1,2,0:T(8,128)(2,1)}, u32[]{:S(2)}) copy-start(bf16[1,8192,8]{1,2,0:T(8,128)(2,1)} %param.16) | copy-start | bytes 393220

commit v2 on v1

--- a/solution.py
+++ b/solution.py
@@ -11,6 +11,7 @@
 SPAN = 64
 LANES = 128
 TILE = 256
+WIDE = 1024
 FEW = 16
 
 epsilon = 1e-05
@@ -99,7 +100,8 @@
             pl.semaphore_signal(
                 barrier, inc=1, device_id={"section": lax.rem(core + k, cores)}, device_id_type=MESH
             )
-        pl.semaphore_wait(barrier, width + groups + cores - 3)
+        with jax.named_scope("barrier"):
+            pl.semaphore_wait(barrier, width + groups + cores - 3)
 
         def a1(k):
             return send(
@@ -235,9 +237,10 @@
         @pl.when(first)
         def _():
             sl[group] = slot_in[...]
-            own_t.wait()
-            for k in in_plane:
-                a1_in(k).wait_recv()
+            with jax.named_scope("a1_wait"):
+                own_t.wait()
+                for k in in_plane:
+                    a1_in(k).wait_recv()
             for k in in_line:
                 a2(k, group).start()
             own_x.start()
@@ -253,23 +256,27 @@
             sc[lane, group] = jnp.broadcast_to(line, (8, LANES))
             for k in in_line:
                 c2(k, group).start()
-            for j in in_line:
-                a2(j, down(j)).wait_recv()
-                for k in in_plane:
-                    a3(j, k, lane).start()
-            for j in in_line:
-                c2(j, down(j)).wait_recv()
+            with jax.named_scope("a2_wait"):
+                for j in in_line:
+                    a2(j, down(j)).wait_recv()
+                    for k in in_plane:
+                        a3(j, k, lane).start()
+            with jax.named_scope("c2_wait"):
+                for j in in_line:
+                    c2(j, down(j)).wait_recv()
             for k in in_plane:
                 c3(k, lane).start()
             for j in in_line:
                 slots(j, down(j)).wait_recv()
-            for k in in_plane:
-                c3(k, left(k)).wait_recv()
-                for j in range(groups):
-                    a3(j, k, left(k)).wait_recv()
-
-        load_in.wait()
-        load_out.wait()
+            with jax.named_scope("a3_wait"):
+                for k in in_plane:
+                    c3(k, left(k)).wait_recv()
+                    for j in range(groups):
+                        a3(j, k, left(k)).wait_recv()
+
+        with jax.named_scope("load_wait"):
+            load_in.wait()
+            load_out.wait()
 
         def permute(c):
             for g in range(groups):
@@ -396,15 +403,17 @@
             normed_s[at : at + SPAN, :] = normed.astype(BF16)
 
         def mix(c):
-            for k in in_line:
-                side_out(c, k).wait_recv()
-                proj_out(c, k).wait_recv()
-            for b in range(spans):
-                scan_span(c, b)
-
-            @pl.loop(0, feats // TILE)
+            with jax.named_scope("y_wait"):
+                for k in in_line:
+                    side_out(c, k).wait_recv()
+                    proj_out(c, k).wait_recv()
+            with jax.named_scope("scan"):
+                for b in range(spans):
+                    scan_span(c, b)
+
+            @pl.loop(0, feats // WIDE)
             def _(n):
-                there = cols(n * TILE, TILE)
+                there = cols(n * WIDE, WIDE)
                 PO[c, :, there] = jnp.dot(
                     normed_s[...], w_out[:, there], preferred_element_type=F32
                 ).astype(BF16)
@@ -413,13 +422,14 @@
                 part_out(c, k).start()
 
         def finish(c):
-            for k in in_plane:
-                part_out(c, k).wait_recv()
-
-            @pl.when(first)
-            def _():
-                for k in in_line:
-                    kept_out(c, k, down(k)).wait_recv()
+            with jax.named_scope("o_wait"):
+                for k in in_plane:
+                    part_out(c, k).wait_recv()
+
+                @pl.when(first)
+                def _():
+                    for k in in_line:
+                        kept_out(c, k, down(k)).wait_recv()
 
             @pl.loop(0, feats // (4 * TILE))
             def _(n):
@@ -438,7 +448,8 @@
             keep(c).start()
 
         def normalise(c):
-            hand_over(c).wait_recv()
+            with jax.named_scope("h_wait"):
+                hand_over(c).wait_recv()
             wide = hin[c].astype(F32)
             scale = lax.rsqrt(jnp.mean(wide * wide, axis=-1, keepdims=True) + epsilon)
             un[c] = (wide * scale * gain[...]).astype(BF16)
@@ -450,56 +461,37 @@
 
         def forward(c):
             for j in in_line:
-                z_out(c, j, down(j)).wait_recv()
+                with jax.named_scope("z_wait"):
+                    z_out(c, j, down(j)).wait_recv()
                 for k in in_plane:
                     spread(c, j, k, lane).start()
 
         def gathered(c):
             for k in in_plane:
-                for j in range(groups):
-                    spread(c, j, k, left(k)).wait_recv()
-
-        mix_lag = jnp.where(first, 2, 1)
-        end_lag = jnp.where(first, 3, 1)
+                with jax.named_scope("g_wait"):
+                    for j in range(groups):
+                        spread(c, j, k, left(k)).wait_recv()
+
+        def when_chunk(index, where, name, step):
+            @pl.when((index >= 0) & (index < chunks) & where)
+            def _():
+                with jax.named_scope(name):
+                    step(index)
+
+        later = jnp.logical_not(first)
+        lag = jnp.where(first, 0, 1)
 
         def turn(i, _):
-            fresh = i < chunks
-
-            @pl.when(fresh & jnp.logical_not(first))
-            def _():
-                normalise(i)
-
-            m = i - mix_lag
-
-            @pl.when((m >= 0) & (m < chunks))
-            def _():
-                mix(m)
-
-            @pl.when(fresh & jnp.logical_not(first))
-            def _():
-                forward(i)
-
-            e = i - end_lag
-
-            @pl.when((e >= 0) & (e < chunks))
-            def _():
-                finish(e)
-
-            @pl.when(fresh & first)
-            def _():
-                permute(i)
-
-            @pl.when(fresh & jnp.logical_not(first))
-            def _():
-                gathered(i)
-
-            @pl.when(fresh)
-            def _():
-                project(i)
-
+            when_chunk(i - 2 - lag, True, "mix", mix)
+            when_chunk(i - 3 - lag, True, "finish", finish)
+            when_chunk(i, later, "normalise", normalise)
+            when_chunk(i, first, "permute", permute)
+            when_chunk(i - 1, later, "gathered", gathered)
+            when_chunk(i - lag, True, "project", project)
+            when_chunk(i, later, "forward", forward)
             return 0
 
-        lax.fori_loop(0, chunks + 3, turn, 0)
+        lax.fori_loop(0, chunks + 4, turn, 0)
 
         def settle(c, _):
             keep(c).wait()

time: 224 us -> 164 us (0.73)
  Pallas kernels: 215 us -> 154 us
    pallas_call x1, Pallas kernels: 215 us -> 154 us  [relay(): pl.pallas_call(kernel, out_shape=jax.ShapeDtypeStruct((row_count, feat_lo...]
where the time goes in v2:
time: 164 us; the launch traced here: 163 us
  Pallas kernels  154 us (94%)
  local copies, waits for them, and re-layouts  7.64 us (5%)
    pallas_call x1, Pallas kernels, relay(): pl.pallas_call(kernel, out_shape=jax.ShapeDtypeStruct((row_count, feat_lo...  154 us

profile of v2, /device:TPU:1, one launch (start us, length us, event | category | flops | bytes accessed | tf_op | source)
XLA Modules:
  0.0 162.7 jit_solution(7135673640339296451)
XLA Ops:
  0.0 0.0 copy-start
  0.0 0.7 convert_element_type.5
  0.7 0.1 reshape.19
  0.8 1.3 copy.12.step_bias
  2.1 1.3 copy.13.a_log
  3.4 0.7 broadcast_in_dim.17
  4.2 0.7 broadcast_in_dim.18.d_skip
  4.8 0.6 broadcast_in_dim.16.rst
  5.4 0.0 copy-done
  5.4 0.6 dynamic-slice_bitcast_fusion.w_step
  6.1 154.3 %shard_map.112 = bf16[256,2048]{1,0:T(8,128)(2,1)} custom-call(bf16[256,2048]{1,0:T(8,128)(2,1)} %tok.1, s32[2,128]{1,0:T(2,128)} %bitcast.16, f32[4,8,128]{2,1,0:T(8,128)} %broadcast_in_dim.16.rst, f32[1,8192]{1,0:T(1,128)} %gain.1, bf16[2048,1280]{1,0:T(8,128)(2,1)} %bitcast.14, bf16[8,2048]{1,0:T(8,128)(2,1)} %dynamic-slice_bitcast_fusion.w_step, ...), custom_call_target="tpu_custom_call" | custom-call | tf_op jit(solution)/shard_map/pallas_call | solution.py:575
  160.4 2.3 %copy.15 = bf16[1,256,2048]{2,1,0:T(8,128)(2,1)} copy(bf16[1,256,2048]{2,1,0:T(8,128)(2,1)} %bitcast.15) | data formatting | bytes 2097152
  (1 shorter events, 0.0 us)
Async XLA Ops:
  0.0 5.4 %copy-start = (bf16[1,8192,8]{1,2,0:T(8,128)(2,1)S(1)}, bf16[1,8192,8]{1,2,0:T(8,128)(2,1)}, u32[]{:S(2)}) copy-start(bf16[1,8192,8]{1,2,0:T(8,128)(2,1)} %param.16) | copy-start | bytes 393220
